TPU v7x, 256 devices: a whole 4x4x8 slice. The times are simulated.
256 devices in a mesh: seq: 32 (over y, x, core), exp: 8 (over z).
Axes of the slice: x: 4, y: 4, z: 8, core: 2. Of those that a mesh axis runs over, the one named last changes fastest.
Arguments:
- queries: bfloat16 [4096, 7168], P('seq', 'exp'), may hold values from -8 to 8
- keys: bfloat16 [4096, 7168], P('seq', 'exp'), may hold values from -8 to 8
- values: bfloat16 [4096, 7168], P('seq', 'exp'), may hold values from -34 to 34
- branch_gates: float32 [4096, 2, 56], P('seq', None, 'exp'), may hold values from 0.1 to 1
- block_choice: int32 [64, 8], P('seq'), may hold values from 0 to 14, as said below
- norm_gain: float32 [7168], P('exp'), may hold values from 0.5 to 1.5
- expert_ids: int32 [4096, 8], P('seq'), may hold values from 0 to 31, all different within a row; in each aligned block of 128 rows (0 to 127, 128 to 255, ...) at most 40 rows name the same one
- route_scores: float32 [4096, 8], P('seq'), may hold values from 0.05 to 1
- w_gate_up: bfloat16 [32, 7168, 2, 1536], P('seq', 'exp'), may hold values from -0.0625 to 0.0625
- w_down: bfloat16 [32, 1536, 7168], P('seq', None, 'exp'), may hold values from -0.15625 to 0.15625
Outputs:
- mixed: bfloat16 [4096, 7168], P('seq', 'exp')
Inputs may be any that keep to these rules, and one draw needn't show every extreme that they name: `block_choice`: each row holds offset 0 and 7 other distinct offsets. `expert_ids`: each row names 8 different experts; within each aligned block of 128 rows (the rows of one index of seq) no expert is named more than 40 times, and that many is reached.
All inputs are finite; a program needn't handle non-finite values.
Results may differ from a plain program's by a relative error of at most 0.029.
Values may be sent and summed in bfloat16 or wider, within the bound.
No kernel may reach another device: no remote copies, remote signals or barrier semaphores. Data moves between devices by JAX's collectives and lax.ppermute only.
A program may use at most 128 MiB of HBM per device.

v0:
```python
import functools

import jax
import jax.numpy as jnp
from jax import lax
from jax.experimental import pallas as pl
from jax.experimental.pallas import tpu as pltpu
from jax.sharding import PartitionSpec as P


HD = 128
D = 7168
BLOCK = 64
EPSILON = 1e-06
ROUTE_SCALE = 2.5
MASKED = -1e30
SUB = 8
PARTS = (24, 16)

f32 = jnp.float32
bf16 = jnp.bfloat16


def mm(a, b, ca, cb):
    return lax.dot_general(a, b, (((ca,), (cb,)), ((), ())), preferred_element_type=f32)


def attention_kernel(
    meta, chosen, ids, route_w, gates, q, *refs, pieces, slots, experts, tokens, heads
):
    kv = refs[:pieces]
    pooled = refs[pieces]
    att_out, slot_out, weight_out = refs[pieces + 1 : pieces + 4]
    x_outs, (bias, cbias, onehot) = refs[pieces + 4 : -3], refs[-3:]
    row = meta[0]
    blocks_here = tokens // BLOCK
    all_blocks = cbias.shape[1]
    scale = HD ** (-0.5)

    q_in = lax.broadcasted_iota(jnp.int32, (tokens, tokens), 0)
    k_in = lax.broadcasted_iota(jnp.int32, (tokens, tokens), 1)
    gap = q_in // BLOCK - k_in // BLOCK
    for p in range(pieces):
        delta = meta[1 + p]
        offset = gap + blocks_here * delta
        hit = offset == chosen[:, 0:1]
        for j in range(1, chosen.shape[1]):
            hit = hit | (offset == chosen[:, j : j + 1])
        ok = hit & (row >= delta)
        if p == 0:
            ok = ok & (k_in <= q_in)
        bias[:, p * tokens : (p + 1) * tokens] = jnp.where(ok, 0.0, MASKED)
    cq = lax.broadcasted_iota(jnp.int32, (tokens, all_blocks), 0) // BLOCK + row * blocks_here
    cb = lax.broadcasted_iota(jnp.int32, (tokens, all_blocks), 1)
    cbias[...] = jnp.where(cb < cq, 0.0, MASKED)
    expert = lax.broadcasted_iota(jnp.int32, (experts, tokens), 0)
    named = jnp.zeros((experts, tokens), f32)
    weight = jnp.zeros((experts, tokens), f32)
    for k in range(ids.shape[0]):
        same = expert == ids[k : k + 1, :]
        named = jnp.where(same, 1.0, named)
        weight = jnp.where(same, route_w[k : k + 1, :], weight)
    before = jnp.where(q_in < k_in, 1.0, 0.0).astype(bf16)
    count = mm(named.astype(bf16), before, 1, 0)
    slot = jnp.where(named > 0.5, count, -1.0)
    slot_out[...] = slot
    weight_out[...] = weight
    base = 0
    for n in slots:
        at = (lax.broadcasted_iota(jnp.int32, (experts, n, tokens), 1) + base).astype(f32)
        hot = jnp.where(slot[:, None, :] == at, 1.0, 0.0)
        onehot[base * experts : (base + n) * experts, :] = hot.reshape(
            experts * n, tokens
        ).astype(bf16)
        base += n

    for h in range(heads):
        at_h = slice(h * HD, (h + 1) * HD)
        qh = q[:, at_h]
        scores = [mm(qh, kv[p][0, :, at_h], 1, 1) for p in range(pieces)]
        s = jnp.concatenate(scores, axis=1) * scale + bias[...]
        top = jnp.max(s, axis=1, keepdims=True)
        w = jnp.exp(s - top)
        total = jnp.sum(w, axis=1, keepdims=True)
        wb = w.astype(bf16)
        fine = mm(wb[:, :tokens], kv[0][1, :, at_h], 1, 0)
        for p in range(1, pieces):
            fine = fine + mm(wb[:, p * tokens : (p + 1) * tokens], kv[p][1, :, at_h], 1, 0)
        cs = mm(qh, pooled[0, :, at_h], 1, 1) * scale + cbias[...]
        ctop = jnp.max(cs, axis=1, keepdims=True)
        ctop = jnp.where(ctop > 0.5 * MASKED, ctop, 0.0)
        cw = jnp.exp(cs - ctop)
        ctotal = jnp.maximum(jnp.sum(cw, axis=1, keepdims=True), 1.0)
        coarse = mm(cw.astype(bf16), pooled[1, :, at_h], 1, 0)
        att = (
            gates[:, h : h + 1] / ctotal * coarse
            + gates[:, heads + h : heads + h + 1] / total * fine
        ).astype(bf16)
        att_out[:, at_h] = att
        base = 0
        for x_out, n in zip(x_outs, slots):
            rows = slice(base * experts, (base + n) * experts)
            x_out[:, at_h] = mm(onehot[rows, :], att, 1, 0).astype(bf16)
            base += n


def attention(meta, chosen, ids, route_w, gates, q, kv, pooled, slots, experts):
    tokens, features = q.shape
    pieces = len(kv)
    all_blocks = pooled.shape[1]
    whole = lambda a: pl.BlockSpec(a.shape, lambda i, m: (0,) * len(a.shape))
    ins = [chosen, ids, route_w, gates, q, *kv, pooled]
    outs = [
        jax.ShapeDtypeStruct((tokens, features), bf16),
        jax.ShapeDtypeStruct((experts, tokens), f32),
        jax.ShapeDtypeStruct((experts, tokens), f32),
        *[jax.ShapeDtypeStruct((experts * n, features), bf16) for n in slots],
    ]
    return pl.pallas_call(
        functools.partial(
            attention_kernel,
            pieces=pieces,
            slots=slots,
            experts=experts,
            tokens=tokens,
            heads=features // HD,
        ),
        name="attend",
        grid_spec=pltpu.PrefetchScalarGridSpec(
            num_scalar_prefetch=1,
            grid=(1,),
            in_specs=[whole(a) for a in ins],
            out_specs=[whole(a) for a in outs],
            scratch_shapes=[
                pltpu.VMEM((tokens, pieces * tokens), f32),
                pltpu.VMEM((tokens, all_blocks), f32),
                pltpu.VMEM((experts * sum(slots), tokens), bf16),
            ],
        ),
        out_shape=outs,
        compiler_params=pltpu.CompilerParams(vmem_limit_bytes=32 << 20),
    )(meta, *ins)


def project_kernel(gain, x, gate_w, up_w, out, scaled, square):
    half = gate_w.shape[1] // out.shape[0]

    @pl.when(pl.program_id(0) == 0)
    def _():
        wide = x[...].astype(f32)
        scaled[...] = (wide * gain[...]).astype(bf16)
        square[...] = mm(
            jnp.ones((SUB, x.shape[1]), bf16), (wide * wide).astype(bf16), 1, 1
        ).astype(bf16)

    gate = mm(gate_w[0], scaled[...], 1, 1).astype(bf16)
    up = mm(up_w[0], scaled[...], 1, 1).astype(bf16)
    for k in range(out.shape[0]):
        out[k, :half, :] = gate[k * half : (k + 1) * half]
        out[k, half : 2 * half, :] = up[k * half : (k + 1) * half]
        out[k, 2 * half :, :] = square[...]


def project(gain, x, w, shards, pair=2):
    _, hidden, features = w.shape
    half = hidden // shards
    rows = x.shape[0]
    return pl.pallas_call(
        project_kernel,
        name="project",
        grid=(shards // pair,),
        in_specs=[
            pl.BlockSpec((1, features), lambda z: (0, 0)),
            pl.BlockSpec((rows, features), lambda z: (0, 0)),
            pl.BlockSpec((1, pair * half, features), lambda z: (0, z, 0)),
            pl.BlockSpec((1, pair * half, features), lambda z: (1, z, 0)),
        ],
        out_specs=pl.BlockSpec((pair, 2 * half + SUB, rows), lambda z: (z, 0, 0)),
        out_shape=jax.ShapeDtypeStruct((shards, 2 * half + SUB, rows), bf16),
        scratch_shapes=[pltpu.VMEM((rows, features), bf16), pltpu.VMEM((SUB, rows), bf16)],
    )(gain, x, w, w)


def activate_kernel(summed, out):
    half = out.shape[0]
    r = lax.rsqrt(summed[2 * half : 2 * half + 1, :].astype(f32) / D + EPSILON)
    gate = summed[:half, :].astype(f32) * r
    up = summed[half : 2 * half, :].astype(f32) * r
    out[...] = (gate / (1.0 + jnp.exp(-gate)) * up).astype(bf16)


def activate(summed, half):
    rows = summed.shape[1]
    return pl.pallas_call(
        activate_kernel,
        name="activate",
        grid=(1,),
        in_specs=[pl.BlockSpec(summed.shape, lambda i: (0, 0))],
        out_specs=pl.BlockSpec((half, rows), lambda i: (0, 0)),
        out_shape=jax.ShapeDtypeStruct((half, rows), bf16),
    )(summed)


def down_kernel(places, *refs):
    acts, (top, bottom, w, out, joined) = refs[:-5], refs[-5:]
    half = acts[0].shape[0]

    def put(k, offset, a):
        start = pl.multiple_of(places[k] * half + offset, 32)
        joined[pl.ds(start, a.shape[0]), :] = a[...]

    for k, a in enumerate(acts):
        put(k, 0, a)
    put(len(acts), 0, top)
    put(len(acts), top.shape[0], bottom)
    out[...] = mm(joined[...], w[...], 0, 0).astype(bf16)


def down(places, acts, w, tile=256):
    rows = acts[0].shape[1]
    hidden, features = w.shape
    return pl.pallas_call(
        down_kernel,
        name="down",
        grid_spec=pltpu.PrefetchScalarGridSpec(
            num_scalar_prefetch=1,
            grid=(rows // tile,),
            in_specs=[pl.BlockSpec((a.shape[0], tile), lambda i, a: (0, i)) for a in acts]
            + [pl.BlockSpec((hidden, features), lambda i, a: (0, 0))],
            out_specs=pl.BlockSpec((tile, features), lambda i, a: (i, 0)),
            scratch_shapes=[pltpu.VMEM((hidden, tile), bf16)],
        ),
        out_shape=jax.ShapeDtypeStruct((rows, features), bf16),
    )(places, *acts, w)


def combine_kernel(slot, weight, x, back, out, *, base, slots):
    experts, tokens = slot.shape
    at = (lax.broadcasted_iota(jnp.int32, (experts, slots, tokens), 1) + base).astype(f32)
    hot = jnp.where(slot[...][:, None, :] == at, weight[...][:, None, :], 0.0)
    mix = hot.reshape(experts * slots, tokens).astype(bf16)
    out[...] = (x[...].astype(f32) + mm(mix, back[...], 0, 0)).astype(out.dtype)


def combine(slot, weight, x, back, base, slots, dtype):
    whole = lambda a: pl.BlockSpec(a.shape, lambda i: (0,) * a.ndim)
    return pl.pallas_call(
        functools.partial(combine_kernel, base=base, slots=slots),
        name="combine",
        grid=(1,),
        in_specs=[whole(slot), whole(weight), whole(x), whole(back)],
        out_specs=whole(x),
        out_shape=jax.ShapeDtypeStruct(x.shape, dtype),
    )(slot, weight, x, back)


def local(
    queries,
    keys,
    values,
    branch_gates,
    block_choice,
    norm_gain,
    expert_ids,
    route_scores,
    w_gate_up,
    w_down,
):
    tokens, features = queries.shape
    blocks_here = tokens // BLOCK
    row = lax.axis_index("seq")
    peers = lax.axis_size("seq")
    me = lax.axis_index("exp")
    ring = lax.axis_size("exp")
    hidden = w_down.shape[1]
    half = hidden // ring

    kv = jnp.stack([keys, values])

    across = 2 * 4
    chip = (row % across) // 2
    odd = row % 2

    def shifted(x, by):
        pairs = [(i, i - i % across + (i + 2 * by) % across) for i in range(peers)]
        return lax.ppermute(x, "seq", pairs)

    def swapped(x):
        return lax.ppermute(x, "seq", [(i, i ^ 1) for i in range(peers)])

    above = lax.ppermute(kv, "seq", [(i, i + across) for i in range(peers - across)])
    far = [shifted(jnp.where(chip >= 4 - by, above, kv), by) for by in (1, 2, 3)]
    beside = swapped(jnp.where(odd == 1, above, kv))
    pieces = [kv, *far, beside, *[swapped(x) for x in far]]
    meta = jnp.stack(
        [row]
        + [jnp.int32(d) for d in (0, 2, 4, 6)]
        + [jnp.where(odd == 1, 1, 7)]
        + [d + 2 * odd for d in (1, 3, 5)]
    ).astype(jnp.int32)
    pooled_here = jnp.mean(
        kv.astype(f32).reshape(2, blocks_here, BLOCK, features), axis=2
    ).astype(bf16)
    copies = jnp.broadcast_to(pooled_here, (peers, *pooled_here.shape))
    everyone = lax.all_to_all(copies, "seq", split_axis=0, concat_axis=0, tiled=True)
    pooled = jnp.transpose(everyone, (1, 0, 2, 3)).reshape(2, peers * blocks_here, features)
    chosen = jnp.repeat(block_choice, BLOCK, axis=0)
    gates = branch_gates.reshape(tokens, -1)
    route_w = ROUTE_SCALE * route_scores / jnp.sum(route_scores, axis=1, keepdims=True)
    w_up = jnp.transpose(w_gate_up[0], (1, 2, 0))
    gain = norm_gain[None, :]
    att, slot, weight, *xs = attention(
        meta, chosen, expert_ids.T, route_w.T, gates, queries, pieces, pooled, PARTS, peers
    )

    def exchanged(x, n):
        return lax.all_to_all(
            x.reshape(peers, n, features), "seq", split_axis=0, concat_axis=0, tiled=True
        ).reshape(peers * n, features)

    to_right = [(i, (i + 1) % ring) for i in range(ring)]
    to_left = [(i, (i - 1) % ring) for i in range(ring)]
    send_right = lambda x: lax.ppermute(x, "exp", to_right)
    send_left = lambda x: lax.ppermute(x, "exp", to_left)
    order = [0, -1, -2, -3, 1, 2, 3, 4]
    places = jnp.stack([(me + k) % ring for k in order]).astype(jnp.int32)
    middle = half // 2
    summed = []
    for x, n in zip(xs, PARTS):
        whole = project(gain, exchanged(x, n), w_up, ring)
        summed.append(
            lax.psum_scatter(whole.reshape(-1, peers * n), "exp", scatter_dimension=0, tiled=True)
        )
    mixed = att
    base = 0
    for c, n in enumerate(PARTS):
        act = activate(summed[c], half)
        rights, lefts = [act], [act]
        for _ in range(3):
            rights.append(send_right(rights[-1]))
            lefts.append(send_left(lefts[-1]))
        top, bottom = send_right(rights[-1][:middle]), send_left(lefts[-1][middle:])
        result = down(places, [*rights, *lefts[1:], top, bottom], w_down[0])
        back = exchanged(result, n)
        last = c == len(PARTS) - 1
        mixed = combine(slot, weight, mixed, back, base, n, bf16 if last else f32)
        base += n
    return mixed


def solution(mesh):
    placed = (
        P("seq", "exp"),
        P("seq", "exp"),
        P("seq", "exp"),
        P("seq", None, "exp"),
        P("seq", None),
        P("exp"),
        P("seq", None),
        P("seq", None),
        P("seq", "exp", None, None),
        P("seq", None, "exp"),
    )

    return jax.shard_map(
        local, mesh=mesh, in_specs=placed, out_specs=P("seq", "exp"), check_vma=False
    )
```

profile of v0, /device:TPU:1, one launch (start us, length us, event | category | flops | bytes accessed | tf_op | source)
XLA Modules:
  0.0 319.4 jit_solution(7848138461789387281)
XLA Ops:
  7.7 4.0 %collective-permute-start = (bf16[2,128,896]{2,1,0:T(8,128)(2,1)S(1)}, bf16[2,128,896]{2,1,0:T(8,128)(2,1)S(1)}, u32[]{:S(2)}, u32[]{:S(2)}) collective-permute-start(bf16[2,128,896]{2,1,0:T(8,128)(2,1)S(1)} %pad_maximum_fusion.refs_0_), channel_id=1, source_target_pairs={{0,64},{8,72},{16,80},{24,88},{32,96},{40,104},{48,112},{56,120},{... | collective-permute-start | bytes 1376264 | tf_op jit(solution)/shard_map/ppermute | solution.py:291
  11.8 9.1 %collective-permute-done = bf16[2,128,896]{2,1,0:T(8,128)(2,1)S(1)} collective-permute-done((bf16[2,128,896]{2,1,0:T(8,128)(2,1)S(1)}, bf16[2,128,896]{2,1,0:T(8,128)(2,1)S(1)}, u32[]{:S(2)}, u32[]{:S(2)}) %collective-permute-start) | collective-permute-done | bytes 458784 | tf_op jit(solution)/shard_map/ppermute | solution.py:291
  30.1 4.6 %collective-permute-done.1.refs_1_ = bf16[2,128,896]{2,1,0:T(8,128)(2,1)S(1)} collective-permute-done((bf16[2,128,896]{2,1,0:T(8,128)(2,1)S(1)}, bf16[2,128,896]{2,1,0:T(8,128)(2,1)S(1)}, u32[]{:S(2)}, u32[]{:S(2)}) %collective-permute-start.1) | collective-permute-done | bytes 458784 | tf_op jit(solution)/shard_map/ppermute | solution.py:286
  38.1 7.4 %collective-permute-done.2.refs_2_ = bf16[2,128,896]{2,1,0:T(8,128)(2,1)S(1)} collective-permute-done((bf16[2,128,896]{2,1,0:T(8,128)(2,1)S(1)}, bf16[2,128,896]{2,1,0:T(8,128)(2,1)S(1)}, u32[]{:S(2)}, u32[]{:S(2)}) %collective-permute-start.2) | collective-permute-done | bytes 458784 | tf_op jit(solution)/shard_map/ppermute | solution.py:286
  48.8 7.7 %all-to-all-start = ((bf16[32,2,2,896]{3,2,1,0:T(2,128)(2,1)}), bf16[32,2,2,896]{3,2,1,0:T(2,128)(2,1)S(1)}, u32[]{:S(2)}, u32[]{:S(2)}) async-start(bf16[32,2,2,896]{3,2,1,0:T(2,128)(2,1)} %broadcast_in_dim.11), calls=%async_computation | async-start | bytes 458752 | tf_op jit(solution)/shard_map/all_to_all | solution.py:305
  56.8 8.3 %all-to-all-done = bf16[32,2,2,896]{3,2,1,0:T(2,128)(2,1)S(1)} async-done(((bf16[32,2,2,896]{3,2,1,0:T(2,128)(2,1)}), bf16[32,2,2,896]{3,2,1,0:T(2,128)(2,1)S(1)}, u32[]{:S(2)}, u32[]{:S(2)}) %all-to-all-start) | async-done | bytes 229408 | tf_op jit(solution)/shard_map/all_to_all | solution.py:305
  71.6 10.1 %attend.1 = (bf16[128,896]{1,0:T(8,128)(2,1)S(1)}, f32[32,128]{1,0:T(8,128)S(1)}, f32[32,128]{1,0:T(8,128)S(1)}, bf16[768,896]{1,0:T(8,128)(2,1)}, bf16[512,896]{1,0:T(8,128)(2,1)S(1)}) custom-call(s32[9]{0:T(128)S(1)} %stack.65.meta, s32[128,8]{1,0:T(8,128)S(1)} %bitcast.39, s32[8,128]{1,0:T(8,128)S(1)} %bitcast.40, ...), custom_call_target="tpu_custom_call" | custom-call | tf_op jit(solution)/shard_map/attend/pallas_call | solution.py:119
  87.6 14.4 %copy.19 = bf16[1,896,2,1536]{1,3,2,0:T(8,128)(2,1)} copy(bf16[1,896,2,1536]{3,2,1,0:T(2,128)(2,1)} %param.18) | data formatting | bytes 11010048 | tf_op args[8]
  102.7 4.5 %all-to-all-done.1 = bf16[32,24,896]{2,1,0:T(8,128)(2,1)S(1)} async-done(((bf16[32,24,896]{2,1,0:T(8,128)(2,1)}), bf16[32,24,896]{2,1,0:T(8,128)(2,1)S(1)}, u32[]{:S(2)}, u32[]{:S(2)}) %all-to-all-start.1) | async-done | bytes 1376288 | tf_op jit(solution)/shard_map/all_to_all | solution.py:317
  108.3 9.4 %project.2 = bf16[8,392,768]{2,1,0:T(8,128)(2,1)} custom-call(f32[1,896]{1,0:T(1,128)} %broadcast_in_dim.12.gain, bf16[768,896]{1,0:T(8,128)(2,1)} %bitcast.51, bf16[2,1536,896]{2,1,0:T(8,128)(2,1)} %bitcast.41, bf16[2,1536,896]{2,1,0:T(8,128)(2,1)} %bitcast.42), custom_call_target="tpu_custom_call" | custom-call | tf_op jit(solution)/shard_map/project/pallas_call | solution.py:168
  117.7 21.0 %all_to_all.25 = bf16[32,16,896]{2,1,0:T(8,128)(2,1)} all-to-all(bf16[32,16,896]{2,1,0:T(8,128)(2,1)S(1)} %bitcast.38), channel_id=1, replica_groups=mesh['seq'=32,'exp'=8] {'seq'}, dimensions={0} | all-to-all | bytes 1835008 | tf_op jit(solution)/shard_map/all_to_all | solution.py:317
  138.7 7.7 %project.3 = bf16[8,392,512]{2,1,0:T(8,128)(2,1)} custom-call(f32[1,896]{1,0:T(1,128)} %broadcast_in_dim.12.gain, bf16[512,896]{1,0:T(8,128)(2,1)} %bitcast.54, bf16[2,1536,896]{2,1,0:T(8,128)(2,1)} %bitcast.43, bf16[2,1536,896]{2,1,0:T(8,128)(2,1)} %bitcast.44), custom_call_target="tpu_custom_call" | custom-call | tf_op jit(solution)/shard_map/project/pallas_call | solution.py:168
  146.4 32.7 %reduce-scatter.3.cloned.1.call-done.summed = bf16[392,768]{1,0:T(8,128)(2,1)} async-done(((bf16[3136,768]{1,0:T(8,128)(2,1)}), bf16[392,768]{1,0:T(8,128)(2,1)}) %reduce-scatter.3.cloned.1.call-update) | async-done | bytes 602128 | tf_op jit(solution)/shard_map/reduce_scatter | solution.py:332
  183.8 6.6 %collective-permute-done.8.refs_1_ = bf16[192,768]{1,0:T(8,128)(2,1)S(1)} collective-permute-done((bf16[192,768]{1,0:T(8,128)(2,1)}, bf16[192,768]{1,0:T(8,128)(2,1)S(1)}, u32[]{:S(2)}, u32[]{:S(2)}) %collective-permute-start.8) | collective-permute-done | bytes 294944 | tf_op jit(solution)/shard_map/ppermute | solution.py:323
  193.0 10.0 %collective-permute-done.9.refs_2_ = bf16[192,768]{1,0:T(8,128)(2,1)S(1)} collective-permute-done((bf16[192,768]{1,0:T(8,128)(2,1)S(1)}, bf16[192,768]{1,0:T(8,128)(2,1)S(1)}, u32[]{:S(2)}, u32[]{:S(2)}) %collective-permute-start.9) | collective-permute-done | bytes 294944 | tf_op jit(solution)/shard_map/ppermute | solution.py:323
  207.5 10.5 %collective-permute-done.10.refs_3_ = bf16[192,768]{1,0:T(8,128)(2,1)S(1)} collective-permute-done((bf16[192,768]{1,0:T(8,128)(2,1)S(1)}, bf16[192,768]{1,0:T(8,128)(2,1)S(1)}, u32[]{:S(2)}, u32[]{:S(2)}) %collective-permute-start.10) | collective-permute-done | bytes 294944 | tf_op jit(solution)/shard_map/ppermute | solution.py:323
  221.8 5.5 %collective-permute-done.14.refs_7_ = bf16[96,768]{1,0:T(8,128)(2,1)S(1)} collective-permute-done((bf16[96,768]{1,0:T(8,128)(2,1)S(1)}, bf16[96,768]{1,0:T(8,128)(2,1)S(1)}, u32[]{:S(2)}, u32[]{:S(2)}) %collective-permute-start.14) | collective-permute-done | bytes 147488 | tf_op jit(solution)/shard_map/ppermute | solution.py:323
  228.0 7.3 %down.2 = bf16[768,896]{1,0:T(8,128)(2,1)} custom-call(s32[8]{0:T(128)} %stack.80.places, bf16[192,768]{1,0:T(8,128)(2,1)} %activate.2.refs_0_, bf16[192,768]{1,0:T(8,128)(2,1)} %copy-done.18, bf16[192,768]{1,0:T(8,128)(2,1)} %copy-done.20, bf16[192,768]{1,0:T(8,128)(2,1)} %copy-done.14, bf16[192,768]{1,0:T(8,128)(2,1)} %copy-done.19, ...), custom_call_target="tpu_custom_call" | custom-call | tf_op jit(solution)/shard_map/down/pallas_call | solution.py:222
  235.3 13.1 %all-to-all-start.2 = ((bf16[32,24,896]{2,1,0:T(8,128)(2,1)}), bf16[32,24,896]{2,1,0:T(8,128)(2,1)S(1)}, u32[]{:S(2)}, u32[]{:S(2)}) async-start(bf16[32,24,896]{2,1,0:T(8,128)(2,1)} %bitcast.49), calls=%async_computation.3 | async-start | bytes 2752512 | tf_op jit(solution)/shard_map/all_to_all | solution.py:317
  253.1 5.1 %collective-permute-done.16.refs_1_ = bf16[192,512]{1,0:T(8,128)(2,1)S(1)} collective-permute-done((bf16[192,512]{1,0:T(8,128)(2,1)}, bf16[192,512]{1,0:T(8,128)(2,1)S(1)}, u32[]{:S(2)}, u32[]{:S(2)}) %collective-permute-start.16) | collective-permute-done | bytes 196640 | tf_op jit(solution)/shard_map/ppermute | solution.py:323
  260.9 4.0 %collective-permute-done.17.refs_2_ = bf16[192,512]{1,0:T(8,128)(2,1)S(1)} collective-permute-done((bf16[192,512]{1,0:T(8,128)(2,1)S(1)}, bf16[192,512]{1,0:T(8,128)(2,1)S(1)}, u32[]{:S(2)}, u32[]{:S(2)}) %collective-permute-start.17) | collective-permute-done | bytes 196640 | tf_op jit(solution)/shard_map/ppermute | solution.py:323
  276.6 5.9 %down.3 = bf16[512,896]{1,0:T(8,128)(2,1)} custom-call(s32[8]{0:T(128)} %stack.80.places, bf16[192,512]{1,0:T(8,128)(2,1)} %activate.3.refs_0_, bf16[192,512]{1,0:T(8,128)(2,1)} %copy-done.22, bf16[192,512]{1,0:T(8,128)(2,1)} %copy-done.24, bf16[192,512]{1,0:T(8,128)(2,1)} %copy-done.16, bf16[192,512]{1,0:T(8,128)(2,1)} %copy-done.23, ...), custom_call_target="tpu_custom_call" | custom-call | tf_op jit(solution)/shard_map/down/pallas_call | solution.py:222
  282.6 11.0 %all-to-all-start.4 = ((bf16[32,16,896]{2,1,0:T(8,128)(2,1)}), bf16[32,16,896]{2,1,0:T(8,128)(2,1)S(1)}, u32[]{:S(2)}, u32[]{:S(2)}) async-start(bf16[32,16,896]{2,1,0:T(8,128)(2,1)} %bitcast.53), calls=%async_computation.6 | async-start | bytes 1835008 | tf_op jit(solution)/shard_map/all_to_all | solution.py:317
  296.3 13.0 %all-to-all-done.4 = bf16[32,16,896]{2,1,0:T(8,128)(2,1)S(1)} async-done(((bf16[32,16,896]{2,1,0:T(8,128)(2,1)}), bf16[32,16,896]{2,1,0:T(8,128)(2,1)S(1)}, u32[]{:S(2)}, u32[]{:S(2)}) %all-to-all-start.4) | async-done | bytes 917536 | tf_op jit(solution)/shard_map/all_to_all | solution.py:317
  (137 shorter events, 72.6 us)
Async XLA Ops:
  7.7 13.2 %collective-permute-start = (bf16[2,128,896]{2,1,0:T(8,128)(2,1)S(1)}, bf16[2,128,896]{2,1,0:T(8,128)(2,1)S(1)}, u32[]{:S(2)}, u32[]{:S(2)}) collective-permute-start(bf16[2,128,896]{2,1,0:T(8,128)(2,1)S(1)} %pad_maximum_fusion.refs_0_), channel_id=1, source_target_pairs={{0,64},{8,72},{16,80},{24,88},{32,96},{40,104},{48,112},{56,120},{... | collective-permute-start | bytes 1376264 | tf_op jit(solution)/shard_map/ppermute | solution.py:291
  22.9 11.8 %collective-permute-start.1 = (bf16[2,128,896]{2,1,0:T(8,128)(2,1)S(1)}, bf16[2,128,896]{2,1,0:T(8,128)(2,1)S(1)}, u32[]{:S(2)}, u32[]{:S(2)}) collective-permute-start(bf16[2,128,896]{2,1,0:T(8,128)(2,1)S(1)} %get-tuple-element.18), channel_id=1, source_target_pairs={{0,16},{8,24},{16,32},{24,40},{32,48},{40,56},{48,0},{56,8},{64,80... | collective-permute-start | bytes 1376264 | tf_op jit(solution)/shard_map/ppermute | solution.py:286
  24.1 21.4 %collective-permute-start.2 = (bf16[2,128,896]{2,1,0:T(8,128)(2,1)S(1)}, bf16[2,128,896]{2,1,0:T(8,128)(2,1)S(1)}, u32[]{:S(2)}, u32[]{:S(2)}) collective-permute-start(bf16[2,128,896]{2,1,0:T(8,128)(2,1)S(1)} %get-tuple-element.17), channel_id=1, source_target_pairs={{0,32},{8,40},{16,48},{24,56},{32,0},{40,8},{48,16},{56,24},{64,96... | collective-permute-start | bytes 1376264 | tf_op jit(solution)/shard_map/ppermute | solution.py:286
  26.6 21.3 %collective-permute-start.3 = (bf16[2,128,896]{2,1,0:T(8,128)(2,1)S(1)}, bf16[2,128,896]{2,1,0:T(8,128)(2,1)S(1)}, u32[]{:S(2)}, u32[]{:S(2)}) collective-permute-start(bf16[2,128,896]{2,1,0:T(8,128)(2,1)S(1)} %get-tuple-element.16), channel_id=1, source_target_pairs={{0,48},{8,56},{16,0},{24,8},{32,16},{40,24},{48,32},{56,40},{64,11... | collective-permute-start | bytes 1376264 | tf_op jit(solution)/shard_map/ppermute | solution.py:286
  27.7 39.3 %collective-permute-start.4 = (bf16[2,128,896]{2,1,0:T(8,128)(2,1)}, bf16[2,128,896]{2,1,0:T(8,128)(2,1)S(1)}, u32[]{:S(2)}, u32[]{:S(2)}) collective-permute-start(bf16[2,128,896]{2,1,0:T(8,128)(2,1)} %get-tuple-element.15), channel_id=1, source_target_pairs={{0,8},{8,0},{16,24},{24,16},{32,40},{40,32},{48,56},{56,48},{64,72... | collective-permute-start | bytes 1376264 | tf_op jit(solution)/shard_map/ppermute | solution.py:289
  34.7 32.3 %collective-permute-start.5 = (bf16[2,128,896]{2,1,0:T(8,128)(2,1)S(1)}, bf16[2,128,896]{2,1,0:T(8,128)(2,1)S(1)}, u32[]{:S(2)}, u32[]{:S(2)}) collective-permute-start(bf16[2,128,896]{2,1,0:T(8,128)(2,1)S(1)} %collective-permute-done.1.refs_1_), channel_id=1, source_target_pairs={{0,8},{8,0},{16,24},{24,16},{32,40},{40,32},{48,56},{56,48},{64,72... | collective-permute-start | bytes 1376264 | tf_op jit(solution)/shard_map/ppermute | solution.py:289
  45.5 22.3 %collective-permute-start.6 = (bf16[2,128,896]{2,1,0:T(8,128)(2,1)S(1)}, bf16[2,128,896]{2,1,0:T(8,128)(2,1)S(1)}, u32[]{:S(2)}, u32[]{:S(2)}) collective-permute-start(bf16[2,128,896]{2,1,0:T(8,128)(2,1)S(1)} %collective-permute-done.2.refs_2_), channel_id=1, source_target_pairs={{0,8},{8,0},{16,24},{24,16},{32,40},{40,32},{48,56},{56,48},{64,72... | collective-permute-start | bytes 1376264 | tf_op jit(solution)/shard_map/ppermute | solution.py:289
  47.9 20.7 %collective-permute-start.7 = (bf16[2,128,896]{2,1,0:T(8,128)(2,1)S(1)}, bf16[2,128,896]{2,1,0:T(8,128)(2,1)}, u32[]{:S(2)}, u32[]{:S(2)}) collective-permute-start(bf16[2,128,896]{2,1,0:T(8,128)(2,1)S(1)} %collective-permute-done.3.refs_3_), channel_id=1, source_target_pairs={{0,8},{8,0},{16,24},{24,16},{32,40},{40,32},{48,56},{56,48},{64,72... | collective-permute-start | bytes 1376264 | tf_op jit(solution)/shard_map/ppermute | solution.py:289
  48.8 16.3 %all-to-all-start = ((bf16[32,2,2,896]{3,2,1,0:T(2,128)(2,1)}), bf16[32,2,2,896]{3,2,1,0:T(2,128)(2,1)S(1)}, u32[]{:S(2)}, u32[]{:S(2)}) async-start(bf16[32,2,2,896]{3,2,1,0:T(2,128)(2,1)} %broadcast_in_dim.11), calls=%async_computation | async-start | bytes 458752 | tf_op jit(solution)/shard_map/all_to_all | solution.py:305
  83.6 23.6 %all-to-all-start.1 = ((bf16[32,24,896]{2,1,0:T(8,128)(2,1)}), bf16[32,24,896]{2,1,0:T(8,128)(2,1)S(1)}, u32[]{:S(2)}, u32[]{:S(2)}) async-start(bf16[32,24,896]{2,1,0:T(8,128)(2,1)} %bitcast.21), calls=%async_computation.1 | async-start | bytes 2752512 | tf_op jit(solution)/shard_map/all_to_all | solution.py:317
  87.4 91.7 %reduce-scatter.3.cloned.1.call-start = ((), (), s32[]{:S(2)}) async-start(), calls=%async_computation.7 | async-start | bytes 5419008 | tf_op jit(solution)/shard_map/reduce_scatter | solution.py:332
  117.7 130.8 %reduce-scatter.5.cloned.1.call-start = ((), (), s32[]{:S(2)}) async-start(), calls=%async_computation.8 | async-start | bytes 3612672 | tf_op jit(solution)/shard_map/reduce_scatter | solution.py:332
  181.1 9.2 %collective-permute-start.8 = (bf16[192,768]{1,0:T(8,128)(2,1)}, bf16[192,768]{1,0:T(8,128)(2,1)S(1)}, u32[]{:S(2)}, u32[]{:S(2)}) collective-permute-start(bf16[192,768]{1,0:T(8,128)(2,1)} %activate.2.refs_0_), channel_id=1, source_target_pairs={{0,1},{1,2},{2,3},{3,4},{4,5},{5,6},{6,7},{7,0},{8,9},{9,10},{10,1... | collective-permute-start | bytes 884744 | tf_op jit(solution)/shard_map/ppermute | solution.py:323
  181.1 9.3 %collective-permute-start.11 = (bf16[192,768]{1,0:T(8,128)(2,1)}, bf16[192,768]{1,0:T(8,128)(2,1)S(1)}, u32[]{:S(2)}, u32[]{:S(2)}) collective-permute-start(bf16[192,768]{1,0:T(8,128)(2,1)} %activate.2.refs_0_), channel_id=1, source_target_pairs={{0,7},{1,0},{2,1},{3,2},{4,3},{5,4},{6,5},{7,6},{8,15},{9,8},{10,9... | collective-permute-start | bytes 884744 | tf_op jit(solution)/shard_map/ppermute | solution.py:324
  190.4 12.6 %collective-permute-start.9 = (bf16[192,768]{1,0:T(8,128)(2,1)S(1)}, bf16[192,768]{1,0:T(8,128)(2,1)S(1)}, u32[]{:S(2)}, u32[]{:S(2)}) collective-permute-start(bf16[192,768]{1,0:T(8,128)(2,1)S(1)} %collective-permute-done.8.refs_1_), channel_id=1, source_target_pairs={{0,1},{1,2},{2,3},{3,4},{4,5},{5,6},{6,7},{7,0},{8,9},{9,10},{10,1... | collective-permute-start | bytes 884744 | tf_op jit(solution)/shard_map/ppermute | solution.py:323
  190.4 13.6 %collective-permute-start.12 = (bf16[192,768]{1,0:T(8,128)(2,1)S(1)}, bf16[192,768]{1,0:T(8,128)(2,1)S(1)}, u32[]{:S(2)}, u32[]{:S(2)}) collective-permute-start(bf16[192,768]{1,0:T(8,128)(2,1)S(1)} %collective-permute-done.11.refs_4_), channel_id=1, source_target_pairs={{0,7},{1,0},{2,1},{3,2},{4,3},{5,4},{6,5},{7,6},{8,15},{9,8},{10,9... | collective-permute-start | bytes 884744 | tf_op jit(solution)/shard_map/ppermute | solution.py:324
  203.0 15.1 %collective-permute-start.10 = (bf16[192,768]{1,0:T(8,128)(2,1)S(1)}, bf16[192,768]{1,0:T(8,128)(2,1)S(1)}, u32[]{:S(2)}, u32[]{:S(2)}) collective-permute-start(bf16[192,768]{1,0:T(8,128)(2,1)S(1)} %collective-permute-done.9.refs_2_), channel_id=1, source_target_pairs={{0,1},{1,2},{2,3},{3,4},{4,5},{5,6},{6,7},{7,0},{8,9},{9,10},{10,1... | collective-permute-start | bytes 884744 | tf_op jit(solution)/shard_map/ppermute | solution.py:323
  204.0 14.2 %collective-permute-start.13 = (bf16[192,768]{1,0:T(8,128)(2,1)S(1)}, bf16[192,768]{1,0:T(8,128)(2,1)S(1)}, u32[]{:S(2)}, u32[]{:S(2)}) collective-permute-start(bf16[192,768]{1,0:T(8,128)(2,1)S(1)} %collective-permute-done.12.refs_5_), channel_id=1, source_target_pairs={{0,7},{1,0},{2,1},{3,2},{4,3},{5,4},{6,5},{7,6},{8,15},{9,8},{10,9... | collective-permute-start | bytes 884744 | tf_op jit(solution)/shard_map/ppermute | solution.py:324
  218.1 9.2 %collective-permute-start.14 = (bf16[96,768]{1,0:T(8,128)(2,1)S(1)}, bf16[96,768]{1,0:T(8,128)(2,1)S(1)}, u32[]{:S(2)}, u32[]{:S(2)}) collective-permute-start(bf16[96,768]{1,0:T(8,128)(2,1)S(1)} %slice.16), channel_id=1, source_target_pairs={{0,1},{1,2},{2,3},{3,4},{4,5},{5,6},{6,7},{7,0},{8,9},{9,10},{10,1... | collective-permute-start | bytes 442376 | tf_op jit(solution)/shard_map/ppermute | solution.py:323
  218.2 9.0 %collective-permute-start.15 = (bf16[96,768]{1,0:T(8,128)(2,1)S(1)}, bf16[96,768]{1,0:T(8,128)(2,1)S(1)}, u32[]{:S(2)}, u32[]{:S(2)}) collective-permute-start(bf16[96,768]{1,0:T(8,128)(2,1)S(1)} %slice.17), channel_id=1, source_target_pairs={{0,7},{1,0},{2,1},{3,2},{4,3},{5,4},{6,5},{7,6},{8,15},{9,8},{10,9... | collective-permute-start | bytes 442376 | tf_op jit(solution)/shard_map/ppermute | solution.py:324
  235.3 47.3 %all-to-all-start.2 = ((bf16[32,24,896]{2,1,0:T(8,128)(2,1)}), bf16[32,24,896]{2,1,0:T(8,128)(2,1)S(1)}, u32[]{:S(2)}, u32[]{:S(2)}) async-start(bf16[32,24,896]{2,1,0:T(8,128)(2,1)} %bitcast.49), calls=%async_computation.3 | async-start | bytes 2752512 | tf_op jit(solution)/shard_map/all_to_all | solution.py:317
  250.3 7.9 %collective-permute-start.16 = (bf16[192,512]{1,0:T(8,128)(2,1)}, bf16[192,512]{1,0:T(8,128)(2,1)S(1)}, u32[]{:S(2)}, u32[]{:S(2)}) collective-permute-start(bf16[192,512]{1,0:T(8,128)(2,1)} %activate.3.refs_0_), channel_id=1, source_target_pairs={{0,1},{1,2},{2,3},{3,4},{4,5},{5,6},{6,7},{7,0},{8,9},{9,10},{10,1... | collective-permute-start | bytes 589832 | tf_op jit(solution)/shard_map/ppermute | solution.py:323
  250.3 7.9 %collective-permute-start.19 = (bf16[192,512]{1,0:T(8,128)(2,1)}, bf16[192,512]{1,0:T(8,128)(2,1)S(1)}, u32[]{:S(2)}, u32[]{:S(2)}) collective-permute-start(bf16[192,512]{1,0:T(8,128)(2,1)} %activate.3.refs_0_), channel_id=1, source_target_pairs={{0,7},{1,0},{2,1},{3,2},{4,3},{5,4},{6,5},{7,6},{8,15},{9,8},{10,9... | collective-permute-start | bytes 589832 | tf_op jit(solution)/shard_map/ppermute | solution.py:324
  282.6 26.7 %all-to-all-start.4 = ((bf16[32,16,896]{2,1,0:T(8,128)(2,1)}), bf16[32,16,896]{2,1,0:T(8,128)(2,1)S(1)}, u32[]{:S(2)}, u32[]{:S(2)}) async-start(bf16[32,16,896]{2,1,0:T(8,128)(2,1)} %bitcast.53), calls=%async_computation.6 | async-start | bytes 1835008 | tf_op jit(solution)/shard_map/all_to_all | solution.py:317
  (40 other events, 575.2 us)
Sparse Core Ops, SparseCore 0:
  117.8 61.2 reduce-scatter.2
  181.7 59.4 reduce-scatter.4
where the time goes:
time: 321 us; the launch traced here: 319 us
  waiting for transfers between devices  127 us (40%)
  starting transfers between devices  75.7 us (24%)
  Pallas kernels  49.4 us (15%)
  local copies, waits for them, and re-layouts  29 us (9%)
  blocking collectives  21 us (7%)
  between operations  13.9 us (4%)
  other arithmetic  3.26 us (1%)
    ppermute x8, waiting for transfers between devices, local(): send_right = lambda x: lax.ppermute(x, 'exp', to_right)  46.6 us
    reduce_scatter x2, waiting for transfers between devices, local(): lax.psum_scatter(whole.reshape(-1, peers * n), 'exp', scatter_dimension=0...  32.7 us
    all_to_all x3, starting transfers between devices, exchanged(): lax.all_to_all(x.reshape(peers, n, features), 'seq', split_axis=0, concat...  27.9 us
    unnamed x70, local copies, waits for them, and re-layouts  24.8 us
    ppermute x8, starting transfers between devices, local(): send_left = lambda x: lax.ppermute(x, 'exp', to_left)  22.6 us
    all_to_all x1, blocking collectives, exchanged(): lax.all_to_all(x.reshape(peers, n, features), 'seq', split_axis=0, concat...  21 us
    all_to_all x3, waiting for transfers between devices, exchanged(): lax.all_to_all(x.reshape(peers, n, features), 'seq', split_axis=0, concat...  17.5 us
    pallas_call x2, Pallas kernels, project(): pl.pallas_call(project_kernel, name='project', grid=(shards // pair,), in...  17.1 us
  transfers between devices with their start and end apart: 30, of which 16 were waited for; matrix products, arithmetic and copies ran while one was open for 6% of the time, Pallas kernels for 9%

commit v1 on v0

--- a/solution.py
+++ b/solution.py
@@ -15,7 +15,7 @@
 ROUTE_SCALE = 2.5
 MASKED = -1e30
 SUB = 8
-PARTS = (24, 16)
+PARTS = (16, 24)
 
 f32 = jnp.float32
 bf16 = jnp.bfloat16
@@ -33,89 +33,93 @@
     att_out, slot_out, weight_out = refs[pieces + 1 : pieces + 4]
     x_outs, (bias, cbias, onehot) = refs[pieces + 4 : -3], refs[-3:]
     row = meta[0]
+    h = pl.program_id(0)
     blocks_here = tokens // BLOCK
     all_blocks = cbias.shape[1]
     scale = HD ** (-0.5)
 
-    q_in = lax.broadcasted_iota(jnp.int32, (tokens, tokens), 0)
-    k_in = lax.broadcasted_iota(jnp.int32, (tokens, tokens), 1)
-    gap = q_in // BLOCK - k_in // BLOCK
-    for p in range(pieces):
-        delta = meta[1 + p]
-        offset = gap + blocks_here * delta
-        hit = offset == chosen[:, 0:1]
-        for j in range(1, chosen.shape[1]):
-            hit = hit | (offset == chosen[:, j : j + 1])
-        ok = hit & (row >= delta)
-        if p == 0:
-            ok = ok & (k_in <= q_in)
-        bias[:, p * tokens : (p + 1) * tokens] = jnp.where(ok, 0.0, MASKED)
-    cq = lax.broadcasted_iota(jnp.int32, (tokens, all_blocks), 0) // BLOCK + row * blocks_here
-    cb = lax.broadcasted_iota(jnp.int32, (tokens, all_blocks), 1)
-    cbias[...] = jnp.where(cb < cq, 0.0, MASKED)
-    expert = lax.broadcasted_iota(jnp.int32, (experts, tokens), 0)
-    named = jnp.zeros((experts, tokens), f32)
-    weight = jnp.zeros((experts, tokens), f32)
-    for k in range(ids.shape[0]):
-        same = expert == ids[k : k + 1, :]
-        named = jnp.where(same, 1.0, named)
-        weight = jnp.where(same, route_w[k : k + 1, :], weight)
-    before = jnp.where(q_in < k_in, 1.0, 0.0).astype(bf16)
-    count = mm(named.astype(bf16), before, 1, 0)
-    slot = jnp.where(named > 0.5, count, -1.0)
-    slot_out[...] = slot
-    weight_out[...] = weight
+    @pl.when(h == 0)
+    def _():
+        q_in = lax.broadcasted_iota(jnp.int32, (tokens, tokens), 0)
+        k_in = lax.broadcasted_iota(jnp.int32, (tokens, tokens), 1)
+        gap = q_in // BLOCK - k_in // BLOCK
+        for p in range(pieces):
+            delta = meta[1 + p]
+            offset = gap + blocks_here * delta
+            hit = offset == chosen[:, 0:1]
+            for j in range(1, chosen.shape[1]):
+                hit = hit | (offset == chosen[:, j : j + 1])
+            ok = hit & (row >= delta)
+            if p == 0:
+                ok = ok & (k_in <= q_in)
+            bias[:, p * tokens : (p + 1) * tokens] = jnp.where(ok, 0.0, MASKED)
+        cq = lax.broadcasted_iota(jnp.int32, (tokens, all_blocks), 0) // BLOCK + row * blocks_here
+        cb = lax.broadcasted_iota(jnp.int32, (tokens, all_blocks), 1)
+        cbias[...] = jnp.where(cb < cq, 0.0, MASKED)
+        expert = lax.broadcasted_iota(jnp.int32, (experts, tokens), 0)
+        named = jnp.zeros((experts, tokens), f32)
+        weight = jnp.zeros((experts, tokens), f32)
+        for k in range(ids.shape[0]):
+            same = expert == ids[k : k + 1, :]
+            named = jnp.where(same, 1.0, named)
+            weight = jnp.where(same, route_w[k : k + 1, :], weight)
+        before = jnp.where(q_in < k_in, 1.0, 0.0).astype(bf16)
+        count = mm(named.astype(bf16), before, 1, 0)
+        slot = jnp.where(named > 0.5, count, -1.0)
+        slot_out[...] = slot
+        weight_out[...] = weight
+        base = 0
+        for n in slots:
+            at = (lax.broadcasted_iota(jnp.int32, (experts, n, tokens), 1) + base).astype(f32)
+            hot = jnp.where(slot[:, None, :] == at, 1.0, 0.0)
+            onehot[base * experts : (base + n) * experts, :] = hot.reshape(
+                experts * n, tokens
+            ).astype(bf16)
+            base += n
+
+    qh = q[...]
+    keys = jnp.concatenate([piece[0] for piece in kv], axis=0)
+    s = mm(qh, keys, 1, 1) * scale + bias[...]
+    top = jnp.max(s, axis=1, keepdims=True)
+    w = jnp.exp(s - top)
+    total = jnp.sum(w, axis=1, keepdims=True)
+    values = jnp.concatenate([piece[1] for piece in kv], axis=0)
+    fine = mm(w.astype(bf16), values, 1, 0)
+    cs = mm(qh, pooled[0], 1, 1) * scale + cbias[...]
+    ctop = jnp.max(cs, axis=1, keepdims=True)
+    ctop = jnp.where(ctop > 0.5 * MASKED, ctop, 0.0)
+    cw = jnp.exp(cs - ctop)
+    ctotal = jnp.maximum(jnp.sum(cw, axis=1, keepdims=True), 1.0)
+    coarse = mm(cw.astype(bf16), pooled[1], 1, 0)
+    lane = lax.broadcasted_iota(jnp.int32, gates.shape, 1)
+    gate_c = jnp.sum(jnp.where(lane == h, gates[...], 0.0), axis=1, keepdims=True)
+    gate_f = jnp.sum(jnp.where(lane == h + heads, gates[...], 0.0), axis=1, keepdims=True)
+    att = (gate_c / ctotal * coarse + gate_f / total * fine).astype(bf16)
+    att_out[...] = att
     base = 0
-    for n in slots:
-        at = (lax.broadcasted_iota(jnp.int32, (experts, n, tokens), 1) + base).astype(f32)
-        hot = jnp.where(slot[:, None, :] == at, 1.0, 0.0)
-        onehot[base * experts : (base + n) * experts, :] = hot.reshape(
-            experts * n, tokens
-        ).astype(bf16)
+    for x_out, n in zip(x_outs, slots):
+        rows = slice(base * experts, (base + n) * experts)
+        x_out[...] = mm(onehot[rows, :], att, 1, 0).astype(bf16)
         base += n
-
-    for h in range(heads):
-        at_h = slice(h * HD, (h + 1) * HD)
-        qh = q[:, at_h]
-        scores = [mm(qh, kv[p][0, :, at_h], 1, 1) for p in range(pieces)]
-        s = jnp.concatenate(scores, axis=1) * scale + bias[...]
-        top = jnp.max(s, axis=1, keepdims=True)
-        w = jnp.exp(s - top)
-        total = jnp.sum(w, axis=1, keepdims=True)
-        wb = w.astype(bf16)
-        fine = mm(wb[:, :tokens], kv[0][1, :, at_h], 1, 0)
-        for p in range(1, pieces):
-            fine = fine + mm(wb[:, p * tokens : (p + 1) * tokens], kv[p][1, :, at_h], 1, 0)
-        cs = mm(qh, pooled[0, :, at_h], 1, 1) * scale + cbias[...]
-        ctop = jnp.max(cs, axis=1, keepdims=True)
-        ctop = jnp.where(ctop > 0.5 * MASKED, ctop, 0.0)
-        cw = jnp.exp(cs - ctop)
-        ctotal = jnp.maximum(jnp.sum(cw, axis=1, keepdims=True), 1.0)
-        coarse = mm(cw.astype(bf16), pooled[1, :, at_h], 1, 0)
-        att = (
-            gates[:, h : h + 1] / ctotal * coarse
-            + gates[:, heads + h : heads + h + 1] / total * fine
-        ).astype(bf16)
-        att_out[:, at_h] = att
-        base = 0
-        for x_out, n in zip(x_outs, slots):
-            rows = slice(base * experts, (base + n) * experts)
-            x_out[:, at_h] = mm(onehot[rows, :], att, 1, 0).astype(bf16)
-            base += n
 
 
 def attention(meta, chosen, ids, route_w, gates, q, kv, pooled, slots, experts):
     tokens, features = q.shape
+    heads = features // HD
     pieces = len(kv)
     all_blocks = pooled.shape[1]
-    whole = lambda a: pl.BlockSpec(a.shape, lambda i, m: (0,) * len(a.shape))
-    ins = [chosen, ids, route_w, gates, q, *kv, pooled]
-    outs = [
-        jax.ShapeDtypeStruct((tokens, features), bf16),
-        jax.ShapeDtypeStruct((experts, tokens), f32),
-        jax.ShapeDtypeStruct((experts, tokens), f32),
-        *[jax.ShapeDtypeStruct((experts * n, features), bf16) for n in slots],
-    ]
+
+    def whole(a):
+        return pl.BlockSpec(a.shape, lambda h, m: (0,) * len(a.shape))
+
+    def per_head(a):
+        zeros = (0,) * (len(a.shape) - 1)
+        return pl.BlockSpec((*a.shape[:-1], HD), lambda h, m: (*zeros, h))
+
+    small = [chosen, ids, route_w, gates]
+    wide = [q, *kv, pooled]
+    table = jax.ShapeDtypeStruct((experts, tokens), f32)
+    dispatched = [jax.ShapeDtypeStruct((experts * n, features), bf16) for n in slots]
     return pl.pallas_call(
         functools.partial(
             attention_kernel,
@@ -123,23 +127,23 @@
             slots=slots,
             experts=experts,
             tokens=tokens,
-            heads=features // HD,
+            heads=heads,
         ),
         name="attend",
         grid_spec=pltpu.PrefetchScalarGridSpec(
             num_scalar_prefetch=1,
-            grid=(1,),
-            in_specs=[whole(a) for a in ins],
-            out_specs=[whole(a) for a in outs],
+            grid=(heads,),
+            in_specs=[whole(a) for a in small] + [per_head(a) for a in wide],
+            out_specs=[per_head(q), whole(table), whole(table)]
+            + [per_head(a) for a in dispatched],
             scratch_shapes=[
                 pltpu.VMEM((tokens, pieces * tokens), f32),
                 pltpu.VMEM((tokens, all_blocks), f32),
                 pltpu.VMEM((experts * sum(slots), tokens), bf16),
             ],
         ),
-        out_shape=outs,
-        compiler_params=pltpu.CompilerParams(vmem_limit_bytes=32 << 20),
-    )(meta, *ins)
+        out_shape=[jax.ShapeDtypeStruct((tokens, features), bf16), table, table, *dispatched],
+    )(meta, *small, *wide)
 
 
 def project_kernel(gain, x, gate_w, up_w, out, scaled, square):

time: 321 us -> 327 us (1.019)
  waiting for transfers between devices: 127 us -> 134 us
  starting transfers between devices: 75.7 us -> 69.3 us
  blocking collectives: 21 us -> 27.4 us
  local copies, waits for them, and re-layouts: 29 us -> 25 us
    reduce_scatter x2, waiting for transfers between devices: 32.7 us -> 61.5 us  [local(): lax.psum_scatter(whole.reshape(-1, peers * n), 'exp', scatter_dimension=0...]
    ppermute x8, waiting for transfers between devices: 46.6 us -> 27.1 us  [local(): send_right = lambda x: lax.ppermute(x, 'exp', to_right)]
    all_to_all x1, blocking collectives: 21 us -> 27.4 us  [exchanged(): lax.all_to_all(x.reshape(peers, n, features), 'seq', split_axis=0, concat...]
    all_to_all x3, starting transfers between devices: 27.9 us -> 22.1 us  [exchanged(): lax.all_to_all(x.reshape(peers, n, features), 'seq', split_axis=0, concat...]
    ppermute x8, starting transfers between devices: 22.6 us -> 17.5 us  [local(): send_left = lambda x: lax.ppermute(x, 'exp', to_left)]
    unnamed x70 -> x66, local copies, waits for them, and re-layouts: 24.8 us -> 19.9 us
    ppermute x8, starting transfers between devices: 0.19 us -> 4.8 us  [local(): send_right = lambda x: lax.ppermute(x, 'exp', to_right)]
  transfers between devices with their start and end apart: 30 -> 30, of which waited for: 16 -> 14; matrix products, arithmetic and copies ran while one was open for 6% -> 6% of each run, Pallas kernels for 9% -> 9%
where the time goes in v1:
time: 327 us; the launch traced here: 325 us
  waiting for transfers between devices  134 us (41%)
  starting transfers between devices  69.3 us (21%)
  Pallas kernels  51 us (16%)
  blocking collectives  27.4 us (8%)
  local copies, waits for them, and re-layouts  25 us (8%)
  between operations  13.9 us (4%)
  other arithmetic  3.88 us (1%)
    reduce_scatter x2, waiting for transfers between devices, local(): lax.psum_scatter(whole.reshape(-1, peers * n), 'exp', scatter_dimension=0...  61.5 us
    all_to_all x1, blocking collectives, exchanged(): lax.all_to_all(x.reshape(peers, n, features), 'seq', split_axis=0, concat...  27.4 us
    ppermute x8, waiting for transfers between devices, local(): send_right = lambda x: lax.ppermute(x, 'exp', to_right)  27.1 us
    all_to_all x3, starting transfers between devices, exchanged(): lax.all_to_all(x.reshape(peers, n, features), 'seq', split_axis=0, concat...  22.1 us
    unnamed x66, local copies, waits for them, and re-layouts  19.9 us
    all_to_all x3, waiting for transfers between devices, exchanged(): lax.all_to_all(x.reshape(peers, n, features), 'seq', split_axis=0, concat...  17.9 us
    ppermute x8, starting transfers between devices, local(): send_left = lambda x: lax.ppermute(x, 'exp', to_left)  17.5 us
    pallas_call x2, Pallas kernels, project(): pl.pallas_call(project_kernel, name='project', grid=(shards // pair,), in...  17.1 us
  transfers between devices with their start and end apart: 30, of which 14 were waited for; matrix products, arithmetic and copies ran while one was open for 6% of the time, Pallas kernels for 9%

profile of v1, /device:TPU:1, one launch (start us, length us, event | category | flops | bytes accessed | tf_op | source)
XLA Modules:
  0.0 324.6 jit_solution(17580115001911587909)
XLA Ops:
  7.7 4.2 %collective-permute-start = (bf16[2,128,896]{2,1,0:T(8,128)(2,1)S(1)}, bf16[2,128,896]{2,1,0:T(8,128)(2,1)S(1)}, u32[]{:S(2)}, u32[]{:S(2)}) collective-permute-start(bf16[2,128,896]{2,1,0:T(8,128)(2,1)S(1)} %pad_maximum_fusion.refs_0_), channel_id=1, source_target_pairs={{0,64},{8,72},{16,80},{24,88},{32,96},{40,104},{48,112},{56,120},{... | collective-permute-start | bytes 1376264 | tf_op jit(solution)/shard_map/ppermute | solution.py:295
  12.0 9.1 %collective-permute-done = bf16[2,128,896]{2,1,0:T(8,128)(2,1)S(1)} collective-permute-done((bf16[2,128,896]{2,1,0:T(8,128)(2,1)S(1)}, bf16[2,128,896]{2,1,0:T(8,128)(2,1)S(1)}, u32[]{:S(2)}, u32[]{:S(2)}) %collective-permute-start) | collective-permute-done | bytes 458784 | tf_op jit(solution)/shard_map/ppermute | solution.py:295
  30.3 4.6 %collective-permute-done.1.refs_1_ = bf16[2,128,896]{2,1,0:T(8,128)(2,1)S(1)} collective-permute-done((bf16[2,128,896]{2,1,0:T(8,128)(2,1)S(1)}, bf16[2,128,896]{2,1,0:T(8,128)(2,1)S(1)}, u32[]{:S(2)}, u32[]{:S(2)}) %collective-permute-start.1) | collective-permute-done | bytes 458784 | tf_op jit(solution)/shard_map/ppermute | solution.py:290
  34.8 3.4 %collective-permute-start.5 = (bf16[2,128,896]{2,1,0:T(8,128)(2,1)S(1)}, bf16[2,128,896]{2,1,0:T(8,128)(2,1)S(1)}, u32[]{:S(2)}, u32[]{:S(2)}) collective-permute-start(bf16[2,128,896]{2,1,0:T(8,128)(2,1)S(1)} %collective-permute-done.1.refs_1_), channel_id=1, source_target_pairs={{0,8},{8,0},{16,24},{24,16},{32,40},{40,32},{48,56},{56,48},{64,72... | collective-permute-start | bytes 1376264 | tf_op jit(solution)/shard_map/ppermute | solution.py:293
  38.2 7.4 %collective-permute-done.2.refs_2_ = bf16[2,128,896]{2,1,0:T(8,128)(2,1)S(1)} collective-permute-done((bf16[2,128,896]{2,1,0:T(8,128)(2,1)S(1)}, bf16[2,128,896]{2,1,0:T(8,128)(2,1)S(1)}, u32[]{:S(2)}, u32[]{:S(2)}) %collective-permute-start.2) | collective-permute-done | bytes 458784 | tf_op jit(solution)/shard_map/ppermute | solution.py:290
  49.1 7.6 %all-to-all-start = ((bf16[32,2,2,896]{3,2,1,0:T(2,128)(2,1)}), bf16[32,2,2,896]{3,2,1,0:T(2,128)(2,1)S(1)}, u32[]{:S(2)}, u32[]{:S(2)}) async-start(bf16[32,2,2,896]{3,2,1,0:T(2,128)(2,1)} %broadcast_in_dim.11), calls=%async_computation | async-start | bytes 458752 | tf_op jit(solution)/shard_map/all_to_all | solution.py:309
  58.7 6.5 %all-to-all-done = bf16[32,2,2,896]{3,2,1,0:T(2,128)(2,1)S(1)} async-done(((bf16[32,2,2,896]{3,2,1,0:T(2,128)(2,1)}), bf16[32,2,2,896]{3,2,1,0:T(2,128)(2,1)S(1)}, u32[]{:S(2)}, u32[]{:S(2)}) %all-to-all-start) | async-done | bytes 229408 | tf_op jit(solution)/shard_map/all_to_all | solution.py:309
  67.2 11.8 %attend.1 = (bf16[128,896]{1,0:T(8,128)(2,1)}, f32[32,128]{1,0:T(8,128)}, f32[32,128]{1,0:T(8,128)}, bf16[512,896]{1,0:T(8,128)(2,1)}, bf16[768,896]{1,0:T(8,128)(2,1)}) custom-call(s32[9]{0:T(128)} %stack.65.meta, s32[128,8]{1,0:T(8,128)} %bitcast.61, s32[8,128]{1,0:T(8,128)} %bitcast.62, f32[8,128]{1,0:T(8,128)} %divide_bitcast_fusion.route_w, ...), custom_call_target="tpu_custom_call" | custom-call | tf_op jit(solution)/shard_map/attend/pallas_call | solution.py:123
  78.9 3.8 %all-to-all-start.1 = ((bf16[32,16,896]{2,1,0:T(8,128)(2,1)}), bf16[32,16,896]{2,1,0:T(8,128)(2,1)S(1)}, u32[]{:S(2)}, u32[]{:S(2)}) async-start(bf16[32,16,896]{2,1,0:T(8,128)(2,1)} %bitcast.59), calls=%async_computation.1 | async-start | bytes 1835008 | tf_op jit(solution)/shard_map/all_to_all | solution.py:321
  83.4 14.4 %copy.19 = bf16[1,896,2,1536]{1,3,2,0:T(8,128)(2,1)} copy(bf16[1,896,2,1536]{3,2,1,0:T(2,128)(2,1)} %param.18) | data formatting | bytes 11010048 | tf_op args[8]
  99.4 7.6 %project.2 = bf16[8,392,512]{2,1,0:T(8,128)(2,1)} custom-call(f32[1,896]{1,0:T(1,128)} %broadcast_in_dim.12.gain, bf16[512,896]{1,0:T(8,128)(2,1)} %bitcast.51, bf16[2,1536,896]{2,1,0:T(8,128)(2,1)} %bitcast.38, bf16[2,1536,896]{2,1,0:T(8,128)(2,1)} %bitcast.39), custom_call_target="tpu_custom_call" | custom-call | tf_op jit(solution)/shard_map/project/pallas_call | solution.py:172
  108.4 27.4 %all_to_all.25 = bf16[32,24,896]{2,1,0:T(8,128)(2,1)} all-to-all(bf16[32,24,896]{2,1,0:T(8,128)(2,1)S(1)} %bitcast.58), channel_id=1, replica_groups=mesh['seq'=32,'exp'=8] {'seq'}, dimensions={0} | all-to-all | bytes 2752512 | tf_op jit(solution)/shard_map/all_to_all | solution.py:321
  135.8 9.4 %project.3 = bf16[8,392,768]{2,1,0:T(8,128)(2,1)} custom-call(f32[1,896]{1,0:T(1,128)} %broadcast_in_dim.12.gain, bf16[768,896]{1,0:T(8,128)(2,1)} %bitcast.48, bf16[2,1536,896]{2,1,0:T(8,128)(2,1)} %bitcast.40, bf16[2,1536,896]{2,1,0:T(8,128)(2,1)} %bitcast.41), custom_call_target="tpu_custom_call" | custom-call | tf_op jit(solution)/shard_map/project/pallas_call | solution.py:172
  145.3 8.6 %reduce-scatter.3.cloned.1.call-done.summed = bf16[392,512]{1,0:T(8,128)(2,1)} async-done(((bf16[3136,512]{1,0:T(8,128)(2,1)}), bf16[392,512]{1,0:T(8,128)(2,1)}) %reduce-scatter.3.cloned.1.call-update) | async-done | bytes 401424 | tf_op jit(solution)/shard_map/reduce_scatter | solution.py:336
  164.3 3.4 %collective-permute-done.9.refs_2_ = bf16[192,512]{1,0:T(8,128)(2,1)S(1)} collective-permute-done((bf16[192,512]{1,0:T(8,128)(2,1)S(1)}, bf16[192,512]{1,0:T(8,128)(2,1)S(1)}, u32[]{:S(2)}, u32[]{:S(2)}) %collective-permute-start.9) | collective-permute-done | bytes 196640 | tf_op jit(solution)/shard_map/ppermute | solution.py:327
  170.6 52.9 %reduce-scatter.5.cloned.1.call-done.summed = bf16[392,768]{1,0:T(8,128)(2,1)} async-done(((bf16[3136,768]{1,0:T(8,128)(2,1)}), bf16[392,768]{1,0:T(8,128)(2,1)}) %reduce-scatter.5.cloned.1.call-update) | async-done | bytes 602128 | tf_op jit(solution)/shard_map/reduce_scatter | solution.py:336
  231.7 5.2 %collective-permute-done.14.refs_7_ = bf16[96,512]{1,0:T(8,128)(2,1)S(1)} collective-permute-done((bf16[96,512]{1,0:T(8,128)(2,1)S(1)}, bf16[96,512]{1,0:T(8,128)(2,1)S(1)}, u32[]{:S(2)}, u32[]{:S(2)}) %collective-permute-start.14) | collective-permute-done | bytes 98336 | tf_op jit(solution)/shard_map/ppermute | solution.py:327
  237.6 5.9 %down.2 = bf16[512,896]{1,0:T(8,128)(2,1)} custom-call(s32[8]{0:T(128)} %stack.80.places, bf16[192,512]{1,0:T(8,128)(2,1)} %activate.2.refs_0_, bf16[192,512]{1,0:T(8,128)(2,1)} %copy-done.20, bf16[192,512]{1,0:T(8,128)(2,1)} %copy-done.22, bf16[192,512]{1,0:T(8,128)(2,1)} %copy-done.14, bf16[192,512]{1,0:T(8,128)(2,1)} %copy-done.21, ...), custom_call_target="tpu_custom_call" | custom-call | tf_op jit(solution)/shard_map/down/pallas_call | solution.py:226
  243.5 8.3 %all-to-all-start.2 = ((bf16[32,16,896]{2,1,0:T(8,128)(2,1)}), bf16[32,16,896]{2,1,0:T(8,128)(2,1)S(1)}, u32[]{:S(2)}, u32[]{:S(2)}) async-start(bf16[32,16,896]{2,1,0:T(8,128)(2,1)} %bitcast.50), calls=%async_computation.3 | async-start | bytes 1835008 | tf_op jit(solution)/shard_map/all_to_all | solution.py:321
  254.7 6.8 %collective-permute-done.17.refs_2_ = bf16[192,768]{1,0:T(8,128)(2,1)S(1)} collective-permute-done((bf16[192,768]{1,0:T(8,128)(2,1)S(1)}, bf16[192,768]{1,0:T(8,128)(2,1)S(1)}, u32[]{:S(2)}, u32[]{:S(2)}) %collective-permute-start.17) | collective-permute-done | bytes 294944 | tf_op jit(solution)/shard_map/ppermute | solution.py:327
  264.2 6.0 %collective-permute-done.18.refs_3_ = bf16[192,768]{1,0:T(8,128)(2,1)S(1)} collective-permute-done((bf16[192,768]{1,0:T(8,128)(2,1)S(1)}, bf16[192,768]{1,0:T(8,128)(2,1)S(1)}, u32[]{:S(2)}, u32[]{:S(2)}) %collective-permute-start.18) | collective-permute-done | bytes 294944 | tf_op jit(solution)/shard_map/ppermute | solution.py:327
  277.0 7.3 %down.3 = bf16[768,896]{1,0:T(8,128)(2,1)} custom-call(s32[8]{0:T(128)} %stack.80.places, bf16[192,768]{1,0:T(8,128)(2,1)} %activate.3.refs_0_, bf16[192,768]{1,0:T(8,128)(2,1)} %copy-done.16, bf16[192,768]{1,0:T(8,128)(2,1)} %copy-done.18, bf16[192,768]{1,0:T(8,128)(2,1)} %copy-done.7, bf16[192,768]{1,0:T(8,128)(2,1)} %copy-done.17, ...), custom_call_target="tpu_custom_call" | custom-call | tf_op jit(solution)/shard_map/down/pallas_call | solution.py:226
  284.3 10.0 %all-to-all-start.4 = ((bf16[32,24,896]{2,1,0:T(8,128)(2,1)}), bf16[32,24,896]{2,1,0:T(8,128)(2,1)S(1)}, u32[]{:S(2)}, u32[]{:S(2)}) async-start(bf16[32,24,896]{2,1,0:T(8,128)(2,1)} %bitcast.46), calls=%async_computation.6 | async-start | bytes 2752512 | tf_op jit(solution)/shard_map/all_to_all | solution.py:321
  296.7 17.3 %all-to-all-done.4 = bf16[32,24,896]{2,1,0:T(8,128)(2,1)S(1)} async-done(((bf16[32,24,896]{2,1,0:T(8,128)(2,1)}), bf16[32,24,896]{2,1,0:T(8,128)(2,1)S(1)}, u32[]{:S(2)}, u32[]{:S(2)}) %all-to-all-start.4) | async-done | bytes 1376288 | tf_op jit(solution)/shard_map/all_to_all | solution.py:321
  (133 shorter events, 61.8 us)
Async XLA Ops:
  7.7 13.3 %collective-permute-start = (bf16[2,128,896]{2,1,0:T(8,128)(2,1)S(1)}, bf16[2,128,896]{2,1,0:T(8,128)(2,1)S(1)}, u32[]{:S(2)}, u32[]{:S(2)}) collective-permute-start(bf16[2,128,896]{2,1,0:T(8,128)(2,1)S(1)} %pad_maximum_fusion.refs_0_), channel_id=1, source_target_pairs={{0,64},{8,72},{16,80},{24,88},{32,96},{40,104},{48,112},{56,120},{... | collective-permute-start | bytes 1376264 | tf_op jit(solution)/shard_map/ppermute | solution.py:295
  23.1 11.8 %collective-permute-start.1 = (bf16[2,128,896]{2,1,0:T(8,128)(2,1)S(1)}, bf16[2,128,896]{2,1,0:T(8,128)(2,1)S(1)}, u32[]{:S(2)}, u32[]{:S(2)}) collective-permute-start(bf16[2,128,896]{2,1,0:T(8,128)(2,1)S(1)} %get-tuple-element.18), channel_id=1, source_target_pairs={{0,16},{8,24},{16,32},{24,40},{32,48},{40,56},{48,0},{56,8},{64,80... | collective-permute-start | bytes 1376264 | tf_op jit(solution)/shard_map/ppermute | solution.py:290
  24.3 21.4 %collective-permute-start.2 = (bf16[2,128,896]{2,1,0:T(8,128)(2,1)S(1)}, bf16[2,128,896]{2,1,0:T(8,128)(2,1)S(1)}, u32[]{:S(2)}, u32[]{:S(2)}) collective-permute-start(bf16[2,128,896]{2,1,0:T(8,128)(2,1)S(1)} %get-tuple-element.17), channel_id=1, source_target_pairs={{0,32},{8,40},{16,48},{24,56},{32,0},{40,8},{48,16},{56,24},{64,96... | collective-permute-start | bytes 1376264 | tf_op jit(solution)/shard_map/ppermute | solution.py:290
  26.7 21.3 %collective-permute-start.3 = (bf16[2,128,896]{2,1,0:T(8,128)(2,1)S(1)}, bf16[2,128,896]{2,1,0:T(8,128)(2,1)S(1)}, u32[]{:S(2)}, u32[]{:S(2)}) collective-permute-start(bf16[2,128,896]{2,1,0:T(8,128)(2,1)S(1)} %get-tuple-element.16), channel_id=1, source_target_pairs={{0,48},{8,56},{16,0},{24,8},{32,16},{40,24},{48,32},{56,40},{64,11... | collective-permute-start | bytes 1376264 | tf_op jit(solution)/shard_map/ppermute | solution.py:290
  27.9 38.3 %collective-permute-start.4 = (bf16[2,128,896]{2,1,0:T(8,128)(2,1)}, bf16[2,128,896]{2,1,0:T(8,128)(2,1)S(1)}, u32[]{:S(2)}, u32[]{:S(2)}) collective-permute-start(bf16[2,128,896]{2,1,0:T(8,128)(2,1)} %get-tuple-element.15), channel_id=1, source_target_pairs={{0,8},{8,0},{16,24},{24,16},{32,40},{40,32},{48,56},{56,48},{64,72... | collective-permute-start | bytes 1376264 | tf_op jit(solution)/shard_map/ppermute | solution.py:293
  34.8 31.4 %collective-permute-start.5 = (bf16[2,128,896]{2,1,0:T(8,128)(2,1)S(1)}, bf16[2,128,896]{2,1,0:T(8,128)(2,1)S(1)}, u32[]{:S(2)}, u32[]{:S(2)}) collective-permute-start(bf16[2,128,896]{2,1,0:T(8,128)(2,1)S(1)} %collective-permute-done.1.refs_1_), channel_id=1, source_target_pairs={{0,8},{8,0},{16,24},{24,16},{32,40},{40,32},{48,56},{56,48},{64,72... | collective-permute-start | bytes 1376264 | tf_op jit(solution)/shard_map/ppermute | solution.py:293
  45.6 20.6 %collective-permute-start.6 = (bf16[2,128,896]{2,1,0:T(8,128)(2,1)S(1)}, bf16[2,128,896]{2,1,0:T(8,128)(2,1)}, u32[]{:S(2)}, u32[]{:S(2)}) collective-permute-start(bf16[2,128,896]{2,1,0:T(8,128)(2,1)S(1)} %collective-permute-done.2.refs_2_), channel_id=1, source_target_pairs={{0,8},{8,0},{16,24},{24,16},{32,40},{40,32},{48,56},{56,48},{64,72... | collective-permute-start | bytes 1376264 | tf_op jit(solution)/shard_map/ppermute | solution.py:293
  48.0 18.2 %collective-permute-start.7 = (bf16[2,128,896]{2,1,0:T(8,128)(2,1)S(1)}, bf16[2,128,896]{2,1,0:T(8,128)(2,1)}, u32[]{:S(2)}, u32[]{:S(2)}) collective-permute-start(bf16[2,128,896]{2,1,0:T(8,128)(2,1)S(1)} %collective-permute-done.3.refs_3_), channel_id=1, source_target_pairs={{0,8},{8,0},{16,24},{24,16},{32,40},{40,32},{48,56},{56,48},{64,72... | collective-permute-start | bytes 1376264 | tf_op jit(solution)/shard_map/ppermute | solution.py:293
  49.1 16.2 %all-to-all-start = ((bf16[32,2,2,896]{3,2,1,0:T(2,128)(2,1)}), bf16[32,2,2,896]{3,2,1,0:T(2,128)(2,1)S(1)}, u32[]{:S(2)}, u32[]{:S(2)}) async-start(bf16[32,2,2,896]{3,2,1,0:T(2,128)(2,1)} %broadcast_in_dim.11), calls=%async_computation | async-start | bytes 458752 | tf_op jit(solution)/shard_map/all_to_all | solution.py:309
  78.9 19.5 %all-to-all-start.1 = ((bf16[32,16,896]{2,1,0:T(8,128)(2,1)}), bf16[32,16,896]{2,1,0:T(8,128)(2,1)S(1)}, u32[]{:S(2)}, u32[]{:S(2)}) async-start(bf16[32,16,896]{2,1,0:T(8,128)(2,1)} %bitcast.59), calls=%async_computation.1 | async-start | bytes 1835008 | tf_op jit(solution)/shard_map/all_to_all | solution.py:321
  82.7 71.1 %reduce-scatter.3.cloned.1.call-start = ((), (), s32[]{:S(2)}) async-start(), calls=%async_computation.7 | async-start | bytes 3612672 | tf_op jit(solution)/shard_map/reduce_scatter | solution.py:336
  107.1 116.4 %reduce-scatter.5.cloned.1.call-start = ((), (), s32[]{:S(2)}) async-start(), calls=%async_computation.8 | async-start | bytes 5419008 | tf_op jit(solution)/shard_map/reduce_scatter | solution.py:336
  167.7 60.5 %collective-permute-start.10 = (bf16[192,512]{1,0:T(8,128)(2,1)S(1)}, bf16[192,512]{1,0:T(8,128)(2,1)S(1)}, u32[]{:S(2)}, u32[]{:S(2)}) collective-permute-start(bf16[192,512]{1,0:T(8,128)(2,1)S(1)} %collective-permute-done.9.refs_2_), channel_id=1, source_target_pairs={{0,1},{1,2},{2,3},{3,4},{4,5},{5,6},{6,7},{7,0},{8,9},{9,10},{10,1... | collective-permute-start | bytes 589832 | tf_op jit(solution)/shard_map/ppermute | solution.py:327
  167.7 60.6 %collective-permute-start.13 = (bf16[192,512]{1,0:T(8,128)(2,1)S(1)}, bf16[192,512]{1,0:T(8,128)(2,1)S(1)}, u32[]{:S(2)}, u32[]{:S(2)}) collective-permute-start(bf16[192,512]{1,0:T(8,128)(2,1)S(1)} %collective-permute-done.12.refs_5_), channel_id=1, source_target_pairs={{0,7},{1,0},{2,1},{3,2},{4,3},{5,4},{6,5},{7,6},{8,15},{9,8},{10,9... | collective-permute-start | bytes 589832 | tf_op jit(solution)/shard_map/ppermute | solution.py:328
  225.5 26.3 %collective-permute-start.16 = (bf16[192,768]{1,0:T(8,128)(2,1)}, bf16[192,768]{1,0:T(8,128)(2,1)S(1)}, u32[]{:S(2)}, u32[]{:S(2)}) collective-permute-start(bf16[192,768]{1,0:T(8,128)(2,1)} %activate.3.refs_0_), channel_id=1, source_target_pairs={{0,1},{1,2},{2,3},{3,4},{4,5},{5,6},{6,7},{7,0},{8,9},{9,10},{10,1... | collective-permute-start | bytes 884744 | tf_op jit(solution)/shard_map/ppermute | solution.py:327
  226.1 28.3 %collective-permute-start.19 = (bf16[192,768]{1,0:T(8,128)(2,1)}, bf16[192,768]{1,0:T(8,128)(2,1)S(1)}, u32[]{:S(2)}, u32[]{:S(2)}) collective-permute-start(bf16[192,768]{1,0:T(8,128)(2,1)} %activate.3.refs_0_), channel_id=1, source_target_pairs={{0,7},{1,0},{2,1},{3,2},{4,3},{5,4},{6,5},{7,6},{8,15},{9,8},{10,9... | collective-permute-start | bytes 884744 | tf_op jit(solution)/shard_map/ppermute | solution.py:328
  228.2 8.6 %collective-permute-start.14 = (bf16[96,512]{1,0:T(8,128)(2,1)S(1)}, bf16[96,512]{1,0:T(8,128)(2,1)S(1)}, u32[]{:S(2)}, u32[]{:S(2)}) collective-permute-start(bf16[96,512]{1,0:T(8,128)(2,1)S(1)} %slice.16), channel_id=1, source_target_pairs={{0,1},{1,2},{2,3},{3,4},{4,5},{5,6},{6,7},{7,0},{8,9},{9,10},{10,1... | collective-permute-start | bytes 294920 | tf_op jit(solution)/shard_map/ppermute | solution.py:327
  228.4 8.5 %collective-permute-start.15 = (bf16[96,512]{1,0:T(8,128)(2,1)S(1)}, bf16[96,512]{1,0:T(8,128)(2,1)S(1)}, u32[]{:S(2)}, u32[]{:S(2)}) collective-permute-start(bf16[96,512]{1,0:T(8,128)(2,1)S(1)} %slice.17), channel_id=1, source_target_pairs={{0,7},{1,0},{2,1},{3,2},{4,3},{5,4},{6,5},{7,6},{8,15},{9,8},{10,9... | collective-permute-start | bytes 294920 | tf_op jit(solution)/shard_map/ppermute | solution.py:328
  243.5 40.8 %all-to-all-start.2 = ((bf16[32,16,896]{2,1,0:T(8,128)(2,1)}), bf16[32,16,896]{2,1,0:T(8,128)(2,1)S(1)}, u32[]{:S(2)}, u32[]{:S(2)}) async-start(bf16[32,16,896]{2,1,0:T(8,128)(2,1)} %bitcast.50), calls=%async_computation.3 | async-start | bytes 1835008 | tf_op jit(solution)/shard_map/all_to_all | solution.py:321
  251.8 9.6 %collective-permute-start.17 = (bf16[192,768]{1,0:T(8,128)(2,1)S(1)}, bf16[192,768]{1,0:T(8,128)(2,1)S(1)}, u32[]{:S(2)}, u32[]{:S(2)}) collective-permute-start(bf16[192,768]{1,0:T(8,128)(2,1)S(1)} %collective-permute-done.16.refs_1_), channel_id=1, source_target_pairs={{0,1},{1,2},{2,3},{3,4},{4,5},{5,6},{6,7},{7,0},{8,9},{9,10},{10,1... | collective-permute-start | bytes 884744 | tf_op jit(solution)/shard_map/ppermute | solution.py:327
  254.4 8.3 %collective-permute-start.20 = (bf16[192,768]{1,0:T(8,128)(2,1)S(1)}, bf16[192,768]{1,0:T(8,128)(2,1)S(1)}, u32[]{:S(2)}, u32[]{:S(2)}) collective-permute-start(bf16[192,768]{1,0:T(8,128)(2,1)S(1)} %collective-permute-done.19.refs_4_), channel_id=1, source_target_pairs={{0,7},{1,0},{2,1},{3,2},{4,3},{5,4},{6,5},{7,6},{8,15},{9,8},{10,9... | collective-permute-start | bytes 884744 | tf_op jit(solution)/shard_map/ppermute | solution.py:328
  261.5 8.7 %collective-permute-start.18 = (bf16[192,768]{1,0:T(8,128)(2,1)S(1)}, bf16[192,768]{1,0:T(8,128)(2,1)S(1)}, u32[]{:S(2)}, u32[]{:S(2)}) collective-permute-start(bf16[192,768]{1,0:T(8,128)(2,1)S(1)} %collective-permute-done.17.refs_2_), channel_id=1, source_target_pairs={{0,1},{1,2},{2,3},{3,4},{4,5},{5,6},{6,7},{7,0},{8,9},{9,10},{10,1... | collective-permute-start | bytes 884744 | tf_op jit(solution)/shard_map/ppermute | solution.py:327
  262.7 7.8 %collective-permute-start.21 = (bf16[192,768]{1,0:T(8,128)(2,1)S(1)}, bf16[192,768]{1,0:T(8,128)(2,1)S(1)}, u32[]{:S(2)}, u32[]{:S(2)}) collective-permute-start(bf16[192,768]{1,0:T(8,128)(2,1)S(1)} %collective-permute-done.20.refs_5_), channel_id=1, source_target_pairs={{0,7},{1,0},{2,1},{3,2},{4,3},{5,4},{6,5},{7,6},{8,15},{9,8},{10,9... | collective-permute-start | bytes 884744 | tf_op jit(solution)/shard_map/ppermute | solution.py:328
  284.3 29.7 %all-to-all-start.4 = ((bf16[32,24,896]{2,1,0:T(8,128)(2,1)}), bf16[32,24,896]{2,1,0:T(8,128)(2,1)S(1)}, u32[]{:S(2)}, u32[]{:S(2)}) async-start(bf16[32,24,896]{2,1,0:T(8,128)(2,1)} %bitcast.46), calls=%async_computation.6 | async-start | bytes 2752512 | tf_op jit(solution)/shard_map/all_to_all | solution.py:321
  (38 other events, 832.0 us)
Sparse Core Ops, SparseCore 0:
  107.2 46.5 reduce-scatter.2
  156.4 67.0 reduce-scatter.4

commit v2 on v0

--- a/solution.py
+++ b/solution.py
@@ -15,7 +15,7 @@
 ROUTE_SCALE = 2.5
 MASKED = -1e30
 SUB = 8
-PARTS = (24, 16)
+PARTS = (16, 24)
 
 f32 = jnp.float32
 bf16 = jnp.bfloat16
@@ -25,18 +25,12 @@
     return lax.dot_general(a, b, (((ca,), (cb,)), ((), ())), preferred_element_type=f32)
 
 
-def attention_kernel(
-    meta, chosen, ids, route_w, gates, q, *refs, pieces, slots, experts, tokens, heads
+def tables_kernel(
+    meta, chosen, ids, route_w, bias, cbias, onehot, slot_out, weight_out, *, pieces, slots
 ):
-    kv = refs[:pieces]
-    pooled = refs[pieces]
-    att_out, slot_out, weight_out = refs[pieces + 1 : pieces + 4]
-    x_outs, (bias, cbias, onehot) = refs[pieces + 4 : -3], refs[-3:]
+    experts, tokens = slot_out.shape
     row = meta[0]
     blocks_here = tokens // BLOCK
-    all_blocks = cbias.shape[1]
-    scale = HD ** (-0.5)
-
     q_in = lax.broadcasted_iota(jnp.int32, (tokens, tokens), 0)
     k_in = lax.broadcasted_iota(jnp.int32, (tokens, tokens), 1)
     gap = q_in // BLOCK - k_in // BLOCK
@@ -50,8 +44,8 @@
         if p == 0:
             ok = ok & (k_in <= q_in)
         bias[:, p * tokens : (p + 1) * tokens] = jnp.where(ok, 0.0, MASKED)
-    cq = lax.broadcasted_iota(jnp.int32, (tokens, all_blocks), 0) // BLOCK + row * blocks_here
-    cb = lax.broadcasted_iota(jnp.int32, (tokens, all_blocks), 1)
+    cq = lax.broadcasted_iota(jnp.int32, cbias.shape, 0) // BLOCK + row * blocks_here
+    cb = lax.broadcasted_iota(jnp.int32, cbias.shape, 1)
     cbias[...] = jnp.where(cb < cq, 0.0, MASKED)
     expert = lax.broadcasted_iota(jnp.int32, (experts, tokens), 0)
     named = jnp.zeros((experts, tokens), f32)
@@ -74,72 +68,91 @@
         ).astype(bf16)
         base += n
 
-    for h in range(heads):
-        at_h = slice(h * HD, (h + 1) * HD)
-        qh = q[:, at_h]
-        scores = [mm(qh, kv[p][0, :, at_h], 1, 1) for p in range(pieces)]
-        s = jnp.concatenate(scores, axis=1) * scale + bias[...]
-        top = jnp.max(s, axis=1, keepdims=True)
-        w = jnp.exp(s - top)
-        total = jnp.sum(w, axis=1, keepdims=True)
-        wb = w.astype(bf16)
-        fine = mm(wb[:, :tokens], kv[0][1, :, at_h], 1, 0)
-        for p in range(1, pieces):
-            fine = fine + mm(wb[:, p * tokens : (p + 1) * tokens], kv[p][1, :, at_h], 1, 0)
-        cs = mm(qh, pooled[0, :, at_h], 1, 1) * scale + cbias[...]
-        ctop = jnp.max(cs, axis=1, keepdims=True)
-        ctop = jnp.where(ctop > 0.5 * MASKED, ctop, 0.0)
-        cw = jnp.exp(cs - ctop)
-        ctotal = jnp.maximum(jnp.sum(cw, axis=1, keepdims=True), 1.0)
-        coarse = mm(cw.astype(bf16), pooled[1, :, at_h], 1, 0)
-        att = (
-            gates[:, h : h + 1] / ctotal * coarse
-            + gates[:, heads + h : heads + h + 1] / total * fine
-        ).astype(bf16)
-        att_out[:, at_h] = att
-        base = 0
-        for x_out, n in zip(x_outs, slots):
-            rows = slice(base * experts, (base + n) * experts)
-            x_out[:, at_h] = mm(onehot[rows, :], att, 1, 0).astype(bf16)
-            base += n
-
-
-def attention(meta, chosen, ids, route_w, gates, q, kv, pooled, slots, experts):
-    tokens, features = q.shape
-    pieces = len(kv)
-    all_blocks = pooled.shape[1]
-    whole = lambda a: pl.BlockSpec(a.shape, lambda i, m: (0,) * len(a.shape))
-    ins = [chosen, ids, route_w, gates, q, *kv, pooled]
+
+def tables(meta, chosen, ids, route_w, pieces, all_blocks, slots, experts):
+    tokens = chosen.shape[0]
+
+    def whole(a):
+        return pl.BlockSpec(a.shape, lambda i, m: (0,) * len(a.shape))
+
     outs = [
-        jax.ShapeDtypeStruct((tokens, features), bf16),
+        jax.ShapeDtypeStruct((tokens, pieces * tokens), f32),
+        jax.ShapeDtypeStruct((tokens, all_blocks), f32),
+        jax.ShapeDtypeStruct((experts * sum(slots), tokens), bf16),
         jax.ShapeDtypeStruct((experts, tokens), f32),
         jax.ShapeDtypeStruct((experts, tokens), f32),
-        *[jax.ShapeDtypeStruct((experts * n, features), bf16) for n in slots],
     ]
     return pl.pallas_call(
-        functools.partial(
-            attention_kernel,
-            pieces=pieces,
-            slots=slots,
-            experts=experts,
-            tokens=tokens,
-            heads=features // HD,
-        ),
-        name="attend",
+        functools.partial(tables_kernel, pieces=pieces, slots=slots),
+        name="tables",
         grid_spec=pltpu.PrefetchScalarGridSpec(
             num_scalar_prefetch=1,
             grid=(1,),
-            in_specs=[whole(a) for a in ins],
+            in_specs=[whole(a) for a in (chosen, ids, route_w)],
             out_specs=[whole(a) for a in outs],
-            scratch_shapes=[
-                pltpu.VMEM((tokens, pieces * tokens), f32),
-                pltpu.VMEM((tokens, all_blocks), f32),
-                pltpu.VMEM((experts * sum(slots), tokens), bf16),
-            ],
         ),
         out_shape=outs,
-        compiler_params=pltpu.CompilerParams(vmem_limit_bytes=32 << 20),
-    )(meta, *ins)
+    )(meta, chosen, ids, route_w)
+
+
+def attention_kernel(bias, cbias, onehot, gates, q, *refs, pieces, slots, experts, heads):
+    kv = refs[:pieces]
+    pooled, att_out, *x_outs = refs[pieces:]
+    h = pl.program_id(0)
+    scale = HD ** (-0.5)
+    qh = q[...]
+    keys = jnp.concatenate([piece[0] for piece in kv], axis=0)
+    s = mm(qh, keys, 1, 1) * scale + bias[...]
+    top = jnp.max(s, axis=1, keepdims=True)
+    w = jnp.exp(s - top)
+    total = jnp.sum(w, axis=1, keepdims=True)
+    values = jnp.concatenate([piece[1] for piece in kv], axis=0)
+    fine = mm(w.astype(bf16), values, 1, 0)
+    cs = mm(qh, pooled[0], 1, 1) * scale + cbias[...]
+    ctop = jnp.max(cs, axis=1, keepdims=True)
+    ctop = jnp.where(ctop > 0.5 * MASKED, ctop, 0.0)
+    cw = jnp.exp(cs - ctop)
+    ctotal = jnp.maximum(jnp.sum(cw, axis=1, keepdims=True), 1.0)
+    coarse = mm(cw.astype(bf16), pooled[1], 1, 0)
+    lane = lax.broadcasted_iota(jnp.int32, gates.shape, 1)
+    gate_c = jnp.sum(jnp.where(lane == h, gates[...], 0.0), axis=1, keepdims=True)
+    gate_f = jnp.sum(jnp.where(lane == h + heads, gates[...], 0.0), axis=1, keepdims=True)
+    att = (gate_c / ctotal * coarse + gate_f / total * fine).astype(bf16)
+    att_out[...] = att
+    base = 0
+    for x_out, n in zip(x_outs, slots):
+        rows = slice(base * experts, (base + n) * experts)
+        x_out[...] = mm(onehot[rows, :], att, 1, 0).astype(bf16)
+        base += n
+
+
+def attention(bias, cbias, onehot, gates, q, kv, pooled, slots, experts):
+    features = q.shape[1]
+    heads = features // HD
+
+    def whole(a):
+        return pl.BlockSpec(a.shape, lambda h: (0,) * len(a.shape))
+
+    def per_head(a):
+        zeros = (0,) * (len(a.shape) - 1)
+        return pl.BlockSpec((*a.shape[:-1], HD), lambda h: (*zeros, h))
+
+    small = [bias, cbias, onehot, gates]
+    wide = [q, *kv, pooled]
+    outs = [
+        jax.ShapeDtypeStruct(q.shape, bf16),
+        *[jax.ShapeDtypeStruct((experts * n, features), bf16) for n in slots],
+    ]
+    return pl.pallas_call(
+        functools.partial(
+            attention_kernel, pieces=len(kv), slots=slots, experts=experts, heads=heads
+        ),
+        name="attend",
+        grid=(heads,),
+        in_specs=[whole(a) for a in small] + [per_head(a) for a in wide],
+        out_specs=[per_head(a) for a in outs],
+        out_shape=outs,
+    )(*small, *wide)
 
 
 def project_kernel(gain, x, gate_w, up_w, out, scaled, square):
@@ -309,9 +322,10 @@
     route_w = ROUTE_SCALE * route_scores / jnp.sum(route_scores, axis=1, keepdims=True)
     w_up = jnp.transpose(w_gate_up[0], (1, 2, 0))
     gain = norm_gain[None, :]
-    att, slot, weight, *xs = attention(
-        meta, chosen, expert_ids.T, route_w.T, gates, queries, pieces, pooled, PARTS, peers
+    bias, cbias, onehot, slot, weight = tables(
+        meta, chosen, expert_ids.T, route_w.T, len(pieces), pooled.shape[1], PARTS, peers
     )
+    att, *xs = attention(bias, cbias, onehot, gates, queries, pieces, pooled, PARTS, peers)
 
     def exchanged(x, n):
         return lax.all_to_all(

time: 321 us -> 327 us (1.019)
  blocking collectives: 21 us -> 27.5 us
  starting transfers between devices: 75.7 us -> 70.4 us
  Pallas kernels: 49.4 us -> 53 us
    reduce_scatter x2, waiting for transfers between devices: 32.7 us -> 61.2 us  [local(): lax.psum_scatter(whole.reshape(-1, peers * n), 'exp', scatter_dimension=0...]
    ppermute x8, waiting for transfers between devices: 46.6 us -> 26.7 us  [local(): send_right = lambda x: lax.ppermute(x, 'exp', to_right)]
    ppermute x8, starting transfers between devices: 22.6 us -> 15.9 us  [local(): send_left = lambda x: lax.ppermute(x, 'exp', to_left)]
    all_to_all x1, blocking collectives: 21 us -> 27.5 us  [exchanged(): lax.all_to_all(x.reshape(peers, n, features), 'seq', split_axis=0, concat...]
    all_to_all x1, waiting for transfers between devices: 8.28 us -> 2.01 us  [local(): lax.all_to_all(copies, 'seq', split_axis=0, concat_axis=0, tiled=True)]
    ppermute x8, starting transfers between devices: 0.19 us -> 6.35 us  [local(): send_right = lambda x: lax.ppermute(x, 'exp', to_right)]
    all_to_all x3, starting transfers between devices: 27.9 us -> 23.3 us  [exchanged(): lax.all_to_all(x.reshape(peers, n, features), 'seq', split_axis=0, concat...]
    unnamed x70 -> x66, local copies, waits for them, and re-layouts: 24.8 us -> 20.7 us
  transfers between devices with their start and end apart: 30 -> 30, of which waited for: 16 -> 15; matrix products, arithmetic and copies ran while one was open for 6% -> 6% of each run, Pallas kernels for 9% -> 10%
where the time goes in v2:
time: 327 us; the launch traced here: 324 us
  waiting for transfers between devices  130 us (40%)
  starting transfers between devices  70.4 us (22%)
  Pallas kernels  53 us (16%)
  blocking collectives  27.5 us (8%)
  local copies, waits for them, and re-layouts  25.8 us (8%)
  between operations  13.8 us (4%)
  other arithmetic  3.86 us (1%)
    reduce_scatter x2, waiting for transfers between devices, local(): lax.psum_scatter(whole.reshape(-1, peers * n), 'exp', scatter_dimension=0...  61.2 us
    all_to_all x1, blocking collectives, exchanged(): lax.all_to_all(x.reshape(peers, n, features), 'seq', split_axis=0, concat...  27.5 us
    ppermute x8, waiting for transfers between devices, local(): send_right = lambda x: lax.ppermute(x, 'exp', to_right)  26.7 us
    all_to_all x3, starting transfers between devices, exchanged(): lax.all_to_all(x.reshape(peers, n, features), 'seq', split_axis=0, concat...  23.3 us
    unnamed x66, local copies, waits for them, and re-layouts  20.7 us
    all_to_all x3, waiting for transfers between devices, exchanged(): lax.all_to_all(x.reshape(peers, n, features), 'seq', split_axis=0, concat...  17.8 us
    pallas_call x2, Pallas kernels, project(): pl.pallas_call(project_kernel, name='project', grid=(shards // pair,), in...  17.1 us
    ppermute x8, starting transfers between devices, local(): send_left = lambda x: lax.ppermute(x, 'exp', to_left)  15.9 us
  transfers between devices with their start and end apart: 30, of which 15 were waited for; matrix products, arithmetic and copies ran while one was open for 6% of the time, Pallas kernels for 10%

profile of v2, /device:TPU:1, one launch (start us, length us, event | category | flops | bytes accessed | tf_op | source)
XLA Modules:
  0.0 324.1 jit_solution(14310168128054560636)
XLA Ops:
  7.7 4.0 %collective-permute-start = (bf16[2,128,896]{2,1,0:T(8,128)(2,1)S(1)}, bf16[2,128,896]{2,1,0:T(8,128)(2,1)S(1)}, u32[]{:S(2)}, u32[]{:S(2)}) collective-permute-start(bf16[2,128,896]{2,1,0:T(8,128)(2,1)S(1)} %pad_maximum_fusion.refs_0_), channel_id=1, source_target_pairs={{0,64},{8,72},{16,80},{24,88},{32,96},{40,104},{48,112},{56,120},{... | collective-permute-start | bytes 1376264 | tf_op jit(solution)/shard_map/ppermute | solution.py:304
  11.8 9.1 %collective-permute-done = bf16[2,128,896]{2,1,0:T(8,128)(2,1)S(1)} collective-permute-done((bf16[2,128,896]{2,1,0:T(8,128)(2,1)S(1)}, bf16[2,128,896]{2,1,0:T(8,128)(2,1)S(1)}, u32[]{:S(2)}, u32[]{:S(2)}) %collective-permute-start) | collective-permute-done | bytes 458784 | tf_op jit(solution)/shard_map/ppermute | solution.py:304
  30.1 4.6 %collective-permute-done.1.refs_1_ = bf16[2,128,896]{2,1,0:T(8,128)(2,1)S(1)} collective-permute-done((bf16[2,128,896]{2,1,0:T(8,128)(2,1)S(1)}, bf16[2,128,896]{2,1,0:T(8,128)(2,1)S(1)}, u32[]{:S(2)}, u32[]{:S(2)}) %collective-permute-start.1) | collective-permute-done | bytes 458784 | tf_op jit(solution)/shard_map/ppermute | solution.py:299
  34.7 3.4 %collective-permute-start.5 = (bf16[2,128,896]{2,1,0:T(8,128)(2,1)S(1)}, bf16[2,128,896]{2,1,0:T(8,128)(2,1)S(1)}, u32[]{:S(2)}, u32[]{:S(2)}) collective-permute-start(bf16[2,128,896]{2,1,0:T(8,128)(2,1)S(1)} %collective-permute-done.1.refs_1_), channel_id=1, source_target_pairs={{0,8},{8,0},{16,24},{24,16},{32,40},{40,32},{48,56},{56,48},{64,72... | collective-permute-start | bytes 1376264 | tf_op jit(solution)/shard_map/ppermute | solution.py:302
  38.1 7.4 %collective-permute-done.2.refs_2_ = bf16[2,128,896]{2,1,0:T(8,128)(2,1)S(1)} collective-permute-done((bf16[2,128,896]{2,1,0:T(8,128)(2,1)S(1)}, bf16[2,128,896]{2,1,0:T(8,128)(2,1)S(1)}, u32[]{:S(2)}, u32[]{:S(2)}) %collective-permute-start.2) | collective-permute-done | bytes 458784 | tf_op jit(solution)/shard_map/ppermute | solution.py:299
  48.9 7.6 %all-to-all-start = ((bf16[32,2,2,896]{3,2,1,0:T(2,128)(2,1)}), bf16[32,2,2,896]{3,2,1,0:T(2,128)(2,1)S(1)}, u32[]{:S(2)}, u32[]{:S(2)}) async-start(bf16[32,2,2,896]{3,2,1,0:T(2,128)(2,1)} %broadcast_in_dim.11), calls=%async_computation | async-start | bytes 458752 | tf_op jit(solution)/shard_map/all_to_all | solution.py:318
  59.3 3.8 %tables.1 = (f32[128,1024]{1,0:T(8,128)}, f32[128,64]{1,0:T(8,128)}, bf16[1280,128]{1,0:T(8,128)(2,1)}, f32[32,128]{1,0:T(8,128)}, f32[32,128]{1,0:T(8,128)}) custom-call(s32[9]{0:T(128)} %stack.65.meta, s32[128,8]{1,0:T(8,128)} %bitcast.61, s32[8,128]{1,0:T(8,128)} %bitcast.62, f32[8,128]{1,0:T(8,128)} %divide_bitcast_fusion.route_w), custom_call_target="tpu_custom_call" | custom-call | tf_op jit(solution)/shard_map/tables/pallas_call | solution.py:85
  67.0 9.9 %attend.1 = (bf16[128,896]{1,0:T(8,128)(2,1)}, bf16[512,896]{1,0:T(8,128)(2,1)}, bf16[768,896]{1,0:T(8,128)(2,1)}) custom-call(f32[128,1024]{1,0:T(8,128)} %get-tuple-element.15.bias, f32[128,64]{1,0:T(8,128)} %get-tuple-element.16.cbias, bf16[1280,128]{1,0:T(8,128)(2,1)} %get-tuple-element.17.onehot, f32[128,14]{1,0:T(8,128)} %copy.18.gates, ...), custom_call_target="tpu_custom_call" | custom-call | tf_op jit(solution)/shard_map/attend/pallas_call | solution.py:146
  76.9 5.4 %all-to-all-start.1 = ((bf16[32,16,896]{2,1,0:T(8,128)(2,1)}), bf16[32,16,896]{2,1,0:T(8,128)(2,1)S(1)}, u32[]{:S(2)}, u32[]{:S(2)}) async-start(bf16[32,16,896]{2,1,0:T(8,128)(2,1)} %bitcast.59), calls=%async_computation.1 | async-start | bytes 1835008 | tf_op jit(solution)/shard_map/all_to_all | solution.py:331
  83.0 14.5 %copy.19 = bf16[1,896,2,1536]{1,3,2,0:T(8,128)(2,1)} copy(bf16[1,896,2,1536]{3,2,1,0:T(2,128)(2,1)} %param.18) | data formatting | bytes 11010048 | tf_op args[8]
  99.0 7.7 %project.2 = bf16[8,392,512]{2,1,0:T(8,128)(2,1)} custom-call(f32[1,896]{1,0:T(1,128)} %broadcast_in_dim.12.gain, bf16[512,896]{1,0:T(8,128)(2,1)} %bitcast.51, bf16[2,1536,896]{2,1,0:T(8,128)(2,1)} %bitcast.38, bf16[2,1536,896]{2,1,0:T(8,128)(2,1)} %bitcast.39), custom_call_target="tpu_custom_call" | custom-call | tf_op jit(solution)/shard_map/project/pallas_call | solution.py:181
  108.0 27.5 %all_to_all.25 = bf16[32,24,896]{2,1,0:T(8,128)(2,1)} all-to-all(bf16[32,24,896]{2,1,0:T(8,128)(2,1)S(1)} %bitcast.58), channel_id=1, replica_groups=mesh['seq'=32,'exp'=8] {'seq'}, dimensions={0} | all-to-all | bytes 2752512 | tf_op jit(solution)/shard_map/all_to_all | solution.py:331
  135.5 9.4 %project.3 = bf16[8,392,768]{2,1,0:T(8,128)(2,1)} custom-call(f32[1,896]{1,0:T(1,128)} %broadcast_in_dim.12.gain, bf16[768,896]{1,0:T(8,128)(2,1)} %bitcast.48, bf16[2,1536,896]{2,1,0:T(8,128)(2,1)} %bitcast.40, bf16[2,1536,896]{2,1,0:T(8,128)(2,1)} %bitcast.41), custom_call_target="tpu_custom_call" | custom-call | tf_op jit(solution)/shard_map/project/pallas_call | solution.py:181
  144.9 8.7 %reduce-scatter.3.cloned.1.call-done.summed = bf16[392,512]{1,0:T(8,128)(2,1)} async-done(((bf16[3136,512]{1,0:T(8,128)(2,1)}), bf16[392,512]{1,0:T(8,128)(2,1)}) %reduce-scatter.3.cloned.1.call-update) | async-done | bytes 401424 | tf_op jit(solution)/shard_map/reduce_scatter | solution.py:346
  158.1 3.3 %collective-permute-done.8.refs_1_ = bf16[192,512]{1,0:T(8,128)(2,1)S(1)} collective-permute-done((bf16[192,512]{1,0:T(8,128)(2,1)}, bf16[192,512]{1,0:T(8,128)(2,1)S(1)}, u32[]{:S(2)}, u32[]{:S(2)}) %collective-permute-start.8) | collective-permute-done | bytes 196640 | tf_op jit(solution)/shard_map/ppermute | solution.py:337
  170.2 52.5 %reduce-scatter.5.cloned.1.call-done.summed = bf16[392,768]{1,0:T(8,128)(2,1)} async-done(((bf16[3136,768]{1,0:T(8,128)(2,1)}), bf16[392,768]{1,0:T(8,128)(2,1)}) %reduce-scatter.5.cloned.1.call-update) | async-done | bytes 602128 | tf_op jit(solution)/shard_map/reduce_scatter | solution.py:346
  231.0 5.0 %collective-permute-done.14.refs_7_ = bf16[96,512]{1,0:T(8,128)(2,1)S(1)} collective-permute-done((bf16[96,512]{1,0:T(8,128)(2,1)S(1)}, bf16[96,512]{1,0:T(8,128)(2,1)S(1)}, u32[]{:S(2)}, u32[]{:S(2)}) %collective-permute-start.14) | collective-permute-done | bytes 98336 | tf_op jit(solution)/shard_map/ppermute | solution.py:337
  237.5 5.9 %down.2 = bf16[512,896]{1,0:T(8,128)(2,1)} custom-call(s32[8]{0:T(128)} %stack.80.places, bf16[192,512]{1,0:T(8,128)(2,1)} %activate.2.refs_0_, bf16[192,512]{1,0:T(8,128)(2,1)} %copy-done.20, bf16[192,512]{1,0:T(8,128)(2,1)} %copy-done.22, bf16[192,512]{1,0:T(8,128)(2,1)} %copy-done.14, bf16[192,512]{1,0:T(8,128)(2,1)} %copy-done.21, ...), custom_call_target="tpu_custom_call" | custom-call | tf_op jit(solution)/shard_map/down/pallas_call | solution.py:235
  243.5 7.9 %all-to-all-start.2 = ((bf16[32,16,896]{2,1,0:T(8,128)(2,1)}), bf16[32,16,896]{2,1,0:T(8,128)(2,1)S(1)}, u32[]{:S(2)}, u32[]{:S(2)}) async-start(bf16[32,16,896]{2,1,0:T(8,128)(2,1)} %bitcast.50), calls=%async_computation.3 | async-start | bytes 1835008 | tf_op jit(solution)/shard_map/all_to_all | solution.py:331
  254.2 6.9 %collective-permute-done.17.refs_2_ = bf16[192,768]{1,0:T(8,128)(2,1)S(1)} collective-permute-done((bf16[192,768]{1,0:T(8,128)(2,1)S(1)}, bf16[192,768]{1,0:T(8,128)(2,1)S(1)}, u32[]{:S(2)}, u32[]{:S(2)}) %collective-permute-start.17) | collective-permute-done | bytes 294944 | tf_op jit(solution)/shard_map/ppermute | solution.py:337
  263.7 6.0 %collective-permute-done.18.refs_3_ = bf16[192,768]{1,0:T(8,128)(2,1)S(1)} collective-permute-done((bf16[192,768]{1,0:T(8,128)(2,1)S(1)}, bf16[192,768]{1,0:T(8,128)(2,1)S(1)}, u32[]{:S(2)}, u32[]{:S(2)}) %collective-permute-start.18) | collective-permute-done | bytes 294944 | tf_op jit(solution)/shard_map/ppermute | solution.py:337
  276.6 7.3 %down.3 = bf16[768,896]{1,0:T(8,128)(2,1)} custom-call(s32[8]{0:T(128)} %stack.80.places, bf16[192,768]{1,0:T(8,128)(2,1)} %activate.3.refs_0_, bf16[192,768]{1,0:T(8,128)(2,1)} %copy-done.16, bf16[192,768]{1,0:T(8,128)(2,1)} %copy-done.18, bf16[192,768]{1,0:T(8,128)(2,1)} %copy-done.7, bf16[192,768]{1,0:T(8,128)(2,1)} %copy-done.17, ...), custom_call_target="tpu_custom_call" | custom-call | tf_op jit(solution)/shard_map/down/pallas_call | solution.py:235
  283.9 9.9 %all-to-all-start.4 = ((bf16[32,24,896]{2,1,0:T(8,128)(2,1)}), bf16[32,24,896]{2,1,0:T(8,128)(2,1)S(1)}, u32[]{:S(2)}, u32[]{:S(2)}) async-start(bf16[32,24,896]{2,1,0:T(8,128)(2,1)} %bitcast.46), calls=%async_computation.6 | async-start | bytes 2752512 | tf_op jit(solution)/shard_map/all_to_all | solution.py:331
  296.3 17.3 %all-to-all-done.4 = bf16[32,24,896]{2,1,0:T(8,128)(2,1)S(1)} async-done(((bf16[32,24,896]{2,1,0:T(8,128)(2,1)}), bf16[32,24,896]{2,1,0:T(8,128)(2,1)S(1)}, u32[]{:S(2)}, u32[]{:S(2)}) %all-to-all-start.4) | async-done | bytes 1376288 | tf_op jit(solution)/shard_map/all_to_all | solution.py:331
  (134 shorter events, 65.3 us)
Async XLA Ops:
  7.7 13.2 %collective-permute-start = (bf16[2,128,896]{2,1,0:T(8,128)(2,1)S(1)}, bf16[2,128,896]{2,1,0:T(8,128)(2,1)S(1)}, u32[]{:S(2)}, u32[]{:S(2)}) collective-permute-start(bf16[2,128,896]{2,1,0:T(8,128)(2,1)S(1)} %pad_maximum_fusion.refs_0_), channel_id=1, source_target_pairs={{0,64},{8,72},{16,80},{24,88},{32,96},{40,104},{48,112},{56,120},{... | collective-permute-start | bytes 1376264 | tf_op jit(solution)/shard_map/ppermute | solution.py:304
  22.9 11.8 %collective-permute-start.1 = (bf16[2,128,896]{2,1,0:T(8,128)(2,1)S(1)}, bf16[2,128,896]{2,1,0:T(8,128)(2,1)S(1)}, u32[]{:S(2)}, u32[]{:S(2)}) collective-permute-start(bf16[2,128,896]{2,1,0:T(8,128)(2,1)S(1)} %get-tuple-element.24), channel_id=1, source_target_pairs={{0,16},{8,24},{16,32},{24,40},{32,48},{40,56},{48,0},{56,8},{64,80... | collective-permute-start | bytes 1376264 | tf_op jit(solution)/shard_map/ppermute | solution.py:299
  24.1 21.4 %collective-permute-start.2 = (bf16[2,128,896]{2,1,0:T(8,128)(2,1)S(1)}, bf16[2,128,896]{2,1,0:T(8,128)(2,1)S(1)}, u32[]{:S(2)}, u32[]{:S(2)}) collective-permute-start(bf16[2,128,896]{2,1,0:T(8,128)(2,1)S(1)} %get-tuple-element.23), channel_id=1, source_target_pairs={{0,32},{8,40},{16,48},{24,56},{32,0},{40,8},{48,16},{56,24},{64,96... | collective-permute-start | bytes 1376264 | tf_op jit(solution)/shard_map/ppermute | solution.py:299
  26.6 21.3 %collective-permute-start.3 = (bf16[2,128,896]{2,1,0:T(8,128)(2,1)S(1)}, bf16[2,128,896]{2,1,0:T(8,128)(2,1)S(1)}, u32[]{:S(2)}, u32[]{:S(2)}) collective-permute-start(bf16[2,128,896]{2,1,0:T(8,128)(2,1)S(1)} %get-tuple-element.22), channel_id=1, source_target_pairs={{0,48},{8,56},{16,0},{24,8},{32,16},{40,24},{48,32},{56,40},{64,11... | collective-permute-start | bytes 1376264 | tf_op jit(solution)/shard_map/ppermute | solution.py:299
  27.7 38.3 %collective-permute-start.4 = (bf16[2,128,896]{2,1,0:T(8,128)(2,1)}, bf16[2,128,896]{2,1,0:T(8,128)(2,1)S(1)}, u32[]{:S(2)}, u32[]{:S(2)}) collective-permute-start(bf16[2,128,896]{2,1,0:T(8,128)(2,1)} %get-tuple-element.21), channel_id=1, source_target_pairs={{0,8},{8,0},{16,24},{24,16},{32,40},{40,32},{48,56},{56,48},{64,72... | collective-permute-start | bytes 1376264 | tf_op jit(solution)/shard_map/ppermute | solution.py:302
  34.7 31.4 %collective-permute-start.5 = (bf16[2,128,896]{2,1,0:T(8,128)(2,1)S(1)}, bf16[2,128,896]{2,1,0:T(8,128)(2,1)S(1)}, u32[]{:S(2)}, u32[]{:S(2)}) collective-permute-start(bf16[2,128,896]{2,1,0:T(8,128)(2,1)S(1)} %collective-permute-done.1.refs_1_), channel_id=1, source_target_pairs={{0,8},{8,0},{16,24},{24,16},{32,40},{40,32},{48,56},{56,48},{64,72... | collective-permute-start | bytes 1376264 | tf_op jit(solution)/shard_map/ppermute | solution.py:302
  45.5 20.6 %collective-permute-start.6 = (bf16[2,128,896]{2,1,0:T(8,128)(2,1)S(1)}, bf16[2,128,896]{2,1,0:T(8,128)(2,1)}, u32[]{:S(2)}, u32[]{:S(2)}) collective-permute-start(bf16[2,128,896]{2,1,0:T(8,128)(2,1)S(1)} %collective-permute-done.2.refs_2_), channel_id=1, source_target_pairs={{0,8},{8,0},{16,24},{24,16},{32,40},{40,32},{48,56},{56,48},{64,72... | collective-permute-start | bytes 1376264 | tf_op jit(solution)/shard_map/ppermute | solution.py:302
  47.9 18.2 %collective-permute-start.7 = (bf16[2,128,896]{2,1,0:T(8,128)(2,1)S(1)}, bf16[2,128,896]{2,1,0:T(8,128)(2,1)}, u32[]{:S(2)}, u32[]{:S(2)}) collective-permute-start(bf16[2,128,896]{2,1,0:T(8,128)(2,1)S(1)} %collective-permute-done.3.refs_3_), channel_id=1, source_target_pairs={{0,8},{8,0},{16,24},{24,16},{32,40},{40,32},{48,56},{56,48},{64,72... | collective-permute-start | bytes 1376264 | tf_op jit(solution)/shard_map/ppermute | solution.py:302
  48.9 16.2 %all-to-all-start = ((bf16[32,2,2,896]{3,2,1,0:T(2,128)(2,1)}), bf16[32,2,2,896]{3,2,1,0:T(2,128)(2,1)S(1)}, u32[]{:S(2)}, u32[]{:S(2)}) async-start(bf16[32,2,2,896]{3,2,1,0:T(2,128)(2,1)} %broadcast_in_dim.11), calls=%async_computation | async-start | bytes 458752 | tf_op jit(solution)/shard_map/all_to_all | solution.py:318
  76.9 21.1 %all-to-all-start.1 = ((bf16[32,16,896]{2,1,0:T(8,128)(2,1)}), bf16[32,16,896]{2,1,0:T(8,128)(2,1)S(1)}, u32[]{:S(2)}, u32[]{:S(2)}) async-start(bf16[32,16,896]{2,1,0:T(8,128)(2,1)} %bitcast.59), calls=%async_computation.1 | async-start | bytes 1835008 | tf_op jit(solution)/shard_map/all_to_all | solution.py:331
  82.3 71.3 %reduce-scatter.3.cloned.1.call-start = ((), (), s32[]{:S(2)}) async-start(), calls=%async_computation.7 | async-start | bytes 3612672 | tf_op jit(solution)/shard_map/reduce_scatter | solution.py:346
  106.7 116.1 %reduce-scatter.5.cloned.1.call-start = ((), (), s32[]{:S(2)}) async-start(), calls=%async_computation.8 | async-start | bytes 5419008 | tf_op jit(solution)/shard_map/reduce_scatter | solution.py:346
  167.3 60.2 %collective-permute-start.10 = (bf16[192,512]{1,0:T(8,128)(2,1)S(1)}, bf16[192,512]{1,0:T(8,128)(2,1)S(1)}, u32[]{:S(2)}, u32[]{:S(2)}) collective-permute-start(bf16[192,512]{1,0:T(8,128)(2,1)S(1)} %collective-permute-done.9.refs_2_), channel_id=1, source_target_pairs={{0,1},{1,2},{2,3},{3,4},{4,5},{5,6},{6,7},{7,0},{8,9},{9,10},{10,1... | collective-permute-start | bytes 589832 | tf_op jit(solution)/shard_map/ppermute | solution.py:337
  167.3 60.7 %collective-permute-start.13 = (bf16[192,512]{1,0:T(8,128)(2,1)S(1)}, bf16[192,512]{1,0:T(8,128)(2,1)S(1)}, u32[]{:S(2)}, u32[]{:S(2)}) collective-permute-start(bf16[192,512]{1,0:T(8,128)(2,1)S(1)} %collective-permute-done.12.refs_5_), channel_id=1, source_target_pairs={{0,7},{1,0},{2,1},{3,2},{4,3},{5,4},{6,5},{7,6},{8,15},{9,8},{10,9... | collective-permute-start | bytes 589832 | tf_op jit(solution)/shard_map/ppermute | solution.py:338
  224.8 26.7 %collective-permute-start.16 = (bf16[192,768]{1,0:T(8,128)(2,1)}, bf16[192,768]{1,0:T(8,128)(2,1)S(1)}, u32[]{:S(2)}, u32[]{:S(2)}) collective-permute-start(bf16[192,768]{1,0:T(8,128)(2,1)} %activate.3.refs_0_), channel_id=1, source_target_pairs={{0,1},{1,2},{2,3},{3,4},{4,5},{5,6},{6,7},{7,0},{8,9},{9,10},{10,1... | collective-permute-start | bytes 884744 | tf_op jit(solution)/shard_map/ppermute | solution.py:337
  225.9 28.3 %collective-permute-start.19 = (bf16[192,768]{1,0:T(8,128)(2,1)}, bf16[192,768]{1,0:T(8,128)(2,1)S(1)}, u32[]{:S(2)}, u32[]{:S(2)}) collective-permute-start(bf16[192,768]{1,0:T(8,128)(2,1)} %activate.3.refs_0_), channel_id=1, source_target_pairs={{0,7},{1,0},{2,1},{3,2},{4,3},{5,4},{6,5},{7,6},{8,15},{9,8},{10,9... | collective-permute-start | bytes 884744 | tf_op jit(solution)/shard_map/ppermute | solution.py:338
  227.5 8.5 %collective-permute-start.14 = (bf16[96,512]{1,0:T(8,128)(2,1)S(1)}, bf16[96,512]{1,0:T(8,128)(2,1)S(1)}, u32[]{:S(2)}, u32[]{:S(2)}) collective-permute-start(bf16[96,512]{1,0:T(8,128)(2,1)S(1)} %slice.16), channel_id=1, source_target_pairs={{0,1},{1,2},{2,3},{3,4},{4,5},{5,6},{6,7},{7,0},{8,9},{9,10},{10,1... | collective-permute-start | bytes 294920 | tf_op jit(solution)/shard_map/ppermute | solution.py:337
  228.0 8.9 %collective-permute-start.15 = (bf16[96,512]{1,0:T(8,128)(2,1)S(1)}, bf16[96,512]{1,0:T(8,128)(2,1)S(1)}, u32[]{:S(2)}, u32[]{:S(2)}) collective-permute-start(bf16[96,512]{1,0:T(8,128)(2,1)S(1)} %slice.17), channel_id=1, source_target_pairs={{0,7},{1,0},{2,1},{3,2},{4,3},{5,4},{6,5},{7,6},{8,15},{9,8},{10,9... | collective-permute-start | bytes 294920 | tf_op jit(solution)/shard_map/ppermute | solution.py:338
  243.5 40.4 %all-to-all-start.2 = ((bf16[32,16,896]{2,1,0:T(8,128)(2,1)}), bf16[32,16,896]{2,1,0:T(8,128)(2,1)S(1)}, u32[]{:S(2)}, u32[]{:S(2)}) async-start(bf16[32,16,896]{2,1,0:T(8,128)(2,1)} %bitcast.50), calls=%async_computation.3 | async-start | bytes 1835008 | tf_op jit(solution)/shard_map/all_to_all | solution.py:331
  251.4 9.6 %collective-permute-start.17 = (bf16[192,768]{1,0:T(8,128)(2,1)S(1)}, bf16[192,768]{1,0:T(8,128)(2,1)S(1)}, u32[]{:S(2)}, u32[]{:S(2)}) collective-permute-start(bf16[192,768]{1,0:T(8,128)(2,1)S(1)} %collective-permute-done.16.refs_1_), channel_id=1, source_target_pairs={{0,1},{1,2},{2,3},{3,4},{4,5},{5,6},{6,7},{7,0},{8,9},{9,10},{10,1... | collective-permute-start | bytes 884744 | tf_op jit(solution)/shard_map/ppermute | solution.py:337
  254.1 8.3 %collective-permute-start.20 = (bf16[192,768]{1,0:T(8,128)(2,1)S(1)}, bf16[192,768]{1,0:T(8,128)(2,1)S(1)}, u32[]{:S(2)}, u32[]{:S(2)}) collective-permute-start(bf16[192,768]{1,0:T(8,128)(2,1)S(1)} %collective-permute-done.19.refs_4_), channel_id=1, source_target_pairs={{0,7},{1,0},{2,1},{3,2},{4,3},{5,4},{6,5},{7,6},{8,15},{9,8},{10,9... | collective-permute-start | bytes 884744 | tf_op jit(solution)/shard_map/ppermute | solution.py:338
  261.1 8.7 %collective-permute-start.18 = (bf16[192,768]{1,0:T(8,128)(2,1)S(1)}, bf16[192,768]{1,0:T(8,128)(2,1)S(1)}, u32[]{:S(2)}, u32[]{:S(2)}) collective-permute-start(bf16[192,768]{1,0:T(8,128)(2,1)S(1)} %collective-permute-done.17.refs_2_), channel_id=1, source_target_pairs={{0,1},{1,2},{2,3},{3,4},{4,5},{5,6},{6,7},{7,0},{8,9},{9,10},{10,1... | collective-permute-start | bytes 884744 | tf_op jit(solution)/shard_map/ppermute | solution.py:337
  262.5 7.8 %collective-permute-start.21 = (bf16[192,768]{1,0:T(8,128)(2,1)S(1)}, bf16[192,768]{1,0:T(8,128)(2,1)S(1)}, u32[]{:S(2)}, u32[]{:S(2)}) collective-permute-start(bf16[192,768]{1,0:T(8,128)(2,1)S(1)} %collective-permute-done.20.refs_5_), channel_id=1, source_target_pairs={{0,7},{1,0},{2,1},{3,2},{4,3},{5,4},{6,5},{7,6},{8,15},{9,8},{10,9... | collective-permute-start | bytes 884744 | tf_op jit(solution)/shard_map/ppermute | solution.py:338
  283.9 29.7 %all-to-all-start.4 = ((bf16[32,24,896]{2,1,0:T(8,128)(2,1)}), bf16[32,24,896]{2,1,0:T(8,128)(2,1)S(1)}, u32[]{:S(2)}, u32[]{:S(2)}) async-start(bf16[32,24,896]{2,1,0:T(8,128)(2,1)} %bitcast.46), calls=%async_computation.6 | async-start | bytes 2752512 | tf_op jit(solution)/shard_map/all_to_all | solution.py:331
  (38 other events, 823.5 us)
Sparse Core Ops, SparseCore 0:
  106.8 46.7 reduce-scatter.2
  156.2 66.4 reduce-scatter.4

commit v3 on v2

--- a/solution.py
+++ b/solution.py
@@ -26,7 +26,7 @@
 
 
 def tables_kernel(
-    meta, chosen, ids, route_w, bias, cbias, onehot, slot_out, weight_out, *, pieces, slots
+    meta, chosen, ids, bias, cbias, onehot, slot_out, *, pieces, slots
 ):
     experts, tokens = slot_out.shape
     row = meta[0]
@@ -49,16 +49,12 @@
     cbias[...] = jnp.where(cb < cq, 0.0, MASKED)
     expert = lax.broadcasted_iota(jnp.int32, (experts, tokens), 0)
     named = jnp.zeros((experts, tokens), f32)
-    weight = jnp.zeros((experts, tokens), f32)
     for k in range(ids.shape[0]):
-        same = expert == ids[k : k + 1, :]
-        named = jnp.where(same, 1.0, named)
-        weight = jnp.where(same, route_w[k : k + 1, :], weight)
+        named = jnp.where(expert == ids[k : k + 1, :], 1.0, named)
     before = jnp.where(q_in < k_in, 1.0, 0.0).astype(bf16)
     count = mm(named.astype(bf16), before, 1, 0)
     slot = jnp.where(named > 0.5, count, -1.0)
     slot_out[...] = slot
-    weight_out[...] = weight
     base = 0
     for n in slots:
         at = (lax.broadcasted_iota(jnp.int32, (experts, n, tokens), 1) + base).astype(f32)
@@ -69,7 +65,7 @@
         base += n
 
 
-def tables(meta, chosen, ids, route_w, pieces, all_blocks, slots, experts):
+def tables(meta, chosen, ids, pieces, all_blocks, slots, experts):
     tokens = chosen.shape[0]
 
     def whole(a):
@@ -80,7 +76,6 @@
         jax.ShapeDtypeStruct((tokens, all_blocks), f32),
         jax.ShapeDtypeStruct((experts * sum(slots), tokens), bf16),
         jax.ShapeDtypeStruct((experts, tokens), f32),
-        jax.ShapeDtypeStruct((experts, tokens), f32),
     ]
     return pl.pallas_call(
         functools.partial(tables_kernel, pieces=pieces, slots=slots),
@@ -88,11 +83,11 @@
         grid_spec=pltpu.PrefetchScalarGridSpec(
             num_scalar_prefetch=1,
             grid=(1,),
-            in_specs=[whole(a) for a in (chosen, ids, route_w)],
+            in_specs=[whole(chosen), whole(ids)],
             out_specs=[whole(a) for a in outs],
         ),
         out_shape=outs,
-    )(meta, chosen, ids, route_w)
+    )(meta, chosen, ids)
 
 
 def attention_kernel(bias, cbias, onehot, gates, q, *refs, pieces, slots, experts, heads):
@@ -247,24 +242,29 @@
     )(places, *acts, w)
 
 
-def combine_kernel(slot, weight, x, back, out, *, base, slots):
+def combine_kernel(slot, ids, scores, x, back, out, *, base, slots):
     experts, tokens = slot.shape
+    route_w = ROUTE_SCALE * scores[...] / jnp.sum(scores[...], axis=0, keepdims=True)
+    expert = lax.broadcasted_iota(jnp.int32, (experts, tokens), 0)
+    weight = jnp.zeros((experts, tokens), f32)
+    for k in range(ids.shape[0]):
+        weight = jnp.where(expert == ids[k : k + 1, :], route_w[k : k + 1, :], weight)
     at = (lax.broadcasted_iota(jnp.int32, (experts, slots, tokens), 1) + base).astype(f32)
-    hot = jnp.where(slot[...][:, None, :] == at, weight[...][:, None, :], 0.0)
+    hot = jnp.where(slot[...][:, None, :] == at, weight[:, None, :], 0.0)
     mix = hot.reshape(experts * slots, tokens).astype(bf16)
     out[...] = (x[...].astype(f32) + mm(mix, back[...], 0, 0)).astype(out.dtype)
 
 
-def combine(slot, weight, x, back, base, slots, dtype):
+def combine(slot, ids, scores, x, back, base, slots, dtype):
     whole = lambda a: pl.BlockSpec(a.shape, lambda i: (0,) * a.ndim)
     return pl.pallas_call(
         functools.partial(combine_kernel, base=base, slots=slots),
         name="combine",
         grid=(1,),
-        in_specs=[whole(slot), whole(weight), whole(x), whole(back)],
+        in_specs=[whole(a) for a in (slot, ids, scores, x, back)],
         out_specs=whole(x),
         out_shape=jax.ShapeDtypeStruct(x.shape, dtype),
-    )(slot, weight, x, back)
+    )(slot, ids, scores, x, back)
 
 
 def local(
@@ -319,11 +319,10 @@
     pooled = jnp.transpose(everyone, (1, 0, 2, 3)).reshape(2, peers * blocks_here, features)
     chosen = jnp.repeat(block_choice, BLOCK, axis=0)
     gates = branch_gates.reshape(tokens, -1)
-    route_w = ROUTE_SCALE * route_scores / jnp.sum(route_scores, axis=1, keepdims=True)
     w_up = jnp.transpose(w_gate_up[0], (1, 2, 0))
     gain = norm_gain[None, :]
-    bias, cbias, onehot, slot, weight = tables(
-        meta, chosen, expert_ids.T, route_w.T, len(pieces), pooled.shape[1], PARTS, peers
+    bias, cbias, onehot, slot = tables(
+        meta, chosen, expert_ids.T, len(pieces), pooled.shape[1], PARTS, peers
     )
     att, *xs = attention(bias, cbias, onehot, gates, queries, pieces, pooled, PARTS, peers)
 
@@ -357,7 +356,9 @@
         result = down(places, [*rights, *lefts[1:], top, bottom], w_down[0])
         back = exchanged(result, n)
         last = c == len(PARTS) - 1
-        mixed = combine(slot, weight, mixed, back, base, n, bf16 if last else f32)
+        mixed = combine(
+            slot, expert_ids.T, route_scores.T, mixed, back, base, n, bf16 if last else f32
+        )
         base += n
     return mixed
 

time: 327 us -> 326 us (level)
    unnamed x66 -> x64, local copies, waits for them, and re-layouts: 20.7 us -> 20.6 us
where the time goes in v3:
time: 326 us; the launch traced here: 324 us
  waiting for transfers between devices  130 us (40%)
  starting transfers between devices  70 us (21%)
  Pallas kernels  53 us (16%)
  blocking collectives  27.5 us (8%)
  local copies, waits for them, and re-layouts  25.7 us (8%)
  between operations  13.8 us (4%)
    reduce_scatter x2, waiting for transfers between devices, local(): lax.psum_scatter(whole.reshape(-1, peers * n), 'exp', scatter_dimension=0...  61.1 us
    all_to_all x1, blocking collectives, exchanged(): lax.all_to_all(x.reshape(peers, n, features), 'seq', split_axis=0, concat...  27.5 us
    ppermute x8, waiting for transfers between devices, local(): send_right = lambda x: lax.ppermute(x, 'exp', to_right)  26.7 us
    all_to_all x3, starting transfers between devices, exchanged(): lax.all_to_all(x.reshape(peers, n, features), 'seq', split_axis=0, concat...  22.9 us
    unnamed x64, local copies, waits for them, and re-layouts  20.6 us
    all_to_all x3, waiting for transfers between devices, exchanged(): lax.all_to_all(x.reshape(peers, n, features), 'seq', split_axis=0, concat...  17.8 us
    pallas_call x2, Pallas kernels, project(): pl.pallas_call(project_kernel, name='project', grid=(shards // pair,), in...  17.1 us
    ppermute x8, starting transfers between devices, local(): send_left = lambda x: lax.ppermute(x, 'exp', to_left)  16.6 us
  transfers between devices with their start and end apart: 30, of which 15 were waited for; matrix products, arithmetic and copies ran while one was open for 6% of the time, Pallas kernels for 10%

profile of v3, /device:TPU:1, one launch (start us, length us, event | category | flops | bytes accessed | tf_op | source)
XLA Modules:
  0.0 323.7 jit_solution(7978353513345597397)
XLA Ops:
  7.7 4.0 %collective-permute-start = (bf16[2,128,896]{2,1,0:T(8,128)(2,1)S(1)}, bf16[2,128,896]{2,1,0:T(8,128)(2,1)S(1)}, u32[]{:S(2)}, u32[]{:S(2)}) collective-permute-start(bf16[2,128,896]{2,1,0:T(8,128)(2,1)S(1)} %pad_maximum_fusion.refs_0_), channel_id=1, source_target_pairs={{0,64},{8,72},{16,80},{24,88},{32,96},{40,104},{48,112},{56,120},{... | collective-permute-start | bytes 1376264 | tf_op jit(solution)/shard_map/ppermute | solution.py:304
  11.8 9.1 %collective-permute-done = bf16[2,128,896]{2,1,0:T(8,128)(2,1)S(1)} collective-permute-done((bf16[2,128,896]{2,1,0:T(8,128)(2,1)S(1)}, bf16[2,128,896]{2,1,0:T(8,128)(2,1)S(1)}, u32[]{:S(2)}, u32[]{:S(2)}) %collective-permute-start) | collective-permute-done | bytes 458784 | tf_op jit(solution)/shard_map/ppermute | solution.py:304
  30.1 4.6 %collective-permute-done.1.refs_1_ = bf16[2,128,896]{2,1,0:T(8,128)(2,1)S(1)} collective-permute-done((bf16[2,128,896]{2,1,0:T(8,128)(2,1)S(1)}, bf16[2,128,896]{2,1,0:T(8,128)(2,1)S(1)}, u32[]{:S(2)}, u32[]{:S(2)}) %collective-permute-start.1) | collective-permute-done | bytes 458784 | tf_op jit(solution)/shard_map/ppermute | solution.py:299
  34.7 3.4 %collective-permute-start.5 = (bf16[2,128,896]{2,1,0:T(8,128)(2,1)S(1)}, bf16[2,128,896]{2,1,0:T(8,128)(2,1)S(1)}, u32[]{:S(2)}, u32[]{:S(2)}) collective-permute-start(bf16[2,128,896]{2,1,0:T(8,128)(2,1)S(1)} %collective-permute-done.1.refs_1_), channel_id=1, source_target_pairs={{0,8},{8,0},{16,24},{24,16},{32,40},{40,32},{48,56},{56,48},{64,72... | collective-permute-start | bytes 1376264 | tf_op jit(solution)/shard_map/ppermute | solution.py:302
  38.1 7.4 %collective-permute-done.2.refs_2_ = bf16[2,128,896]{2,1,0:T(8,128)(2,1)S(1)} collective-permute-done((bf16[2,128,896]{2,1,0:T(8,128)(2,1)S(1)}, bf16[2,128,896]{2,1,0:T(8,128)(2,1)S(1)}, u32[]{:S(2)}, u32[]{:S(2)}) %collective-permute-start.2) | collective-permute-done | bytes 458784 | tf_op jit(solution)/shard_map/ppermute | solution.py:299
  48.9 7.6 %all-to-all-start = ((bf16[32,2,2,896]{3,2,1,0:T(2,128)(2,1)}), bf16[32,2,2,896]{3,2,1,0:T(2,128)(2,1)S(1)}, u32[]{:S(2)}, u32[]{:S(2)}) async-start(bf16[32,2,2,896]{3,2,1,0:T(2,128)(2,1)} %broadcast_in_dim.10), calls=%async_computation | async-start | bytes 458752 | tf_op jit(solution)/shard_map/all_to_all | solution.py:318
  58.6 3.8 %tables.1 = (f32[128,1024]{1,0:T(8,128)}, f32[128,64]{1,0:T(8,128)}, bf16[1280,128]{1,0:T(8,128)(2,1)}, f32[32,128]{1,0:T(8,128)}) custom-call(s32[9]{0:T(128)} %stack.65.meta, s32[128,8]{1,0:T(8,128)} %bitcast.60, s32[8,128]{1,0:T(8,128)} %bitcast.61), custom_call_target="tpu_custom_call" | custom-call | tf_op jit(solution)/shard_map/tables/pallas_call | solution.py:80
  67.0 9.9 %attend.1 = (bf16[128,896]{1,0:T(8,128)(2,1)}, bf16[512,896]{1,0:T(8,128)(2,1)}, bf16[768,896]{1,0:T(8,128)(2,1)}) custom-call(f32[128,1024]{1,0:T(8,128)} %get-tuple-element.13.bias, f32[128,64]{1,0:T(8,128)} %get-tuple-element.14.cbias, bf16[1280,128]{1,0:T(8,128)(2,1)} %get-tuple-element.15.onehot, f32[128,14]{1,0:T(8,128)} %copy.18.gates, ...), custom_call_target="tpu_custom_call" | custom-call | tf_op jit(solution)/shard_map/attend/pallas_call | solution.py:141
  76.9 4.7 %all-to-all-start.1 = ((bf16[32,16,896]{2,1,0:T(8,128)(2,1)}), bf16[32,16,896]{2,1,0:T(8,128)(2,1)S(1)}, u32[]{:S(2)}, u32[]{:S(2)}) async-start(bf16[32,16,896]{2,1,0:T(8,128)(2,1)} %bitcast.58), calls=%async_computation.1 | async-start | bytes 1835008 | tf_op jit(solution)/shard_map/all_to_all | solution.py:330
  82.3 14.4 %copy.19 = bf16[1,896,2,1536]{1,3,2,0:T(8,128)(2,1)} copy(bf16[1,896,2,1536]{3,2,1,0:T(2,128)(2,1)} %param.18) | data formatting | bytes 11010048 | tf_op args[8]
  98.3 7.6 %project.2 = bf16[8,392,512]{2,1,0:T(8,128)(2,1)} custom-call(f32[1,896]{1,0:T(1,128)} %broadcast_in_dim.11.gain, bf16[512,896]{1,0:T(8,128)(2,1)} %bitcast.50, bf16[2,1536,896]{2,1,0:T(8,128)(2,1)} %bitcast.37, bf16[2,1536,896]{2,1,0:T(8,128)(2,1)} %bitcast.38), custom_call_target="tpu_custom_call" | custom-call | tf_op jit(solution)/shard_map/project/pallas_call | solution.py:176
  107.3 27.5 %all_to_all.25 = bf16[32,24,896]{2,1,0:T(8,128)(2,1)} all-to-all(bf16[32,24,896]{2,1,0:T(8,128)(2,1)S(1)} %bitcast.57), channel_id=1, replica_groups=mesh['seq'=32,'exp'=8] {'seq'}, dimensions={0} | all-to-all | bytes 2752512 | tf_op jit(solution)/shard_map/all_to_all | solution.py:330
  134.8 9.5 %project.3 = bf16[8,392,768]{2,1,0:T(8,128)(2,1)} custom-call(f32[1,896]{1,0:T(1,128)} %broadcast_in_dim.11.gain, bf16[768,896]{1,0:T(8,128)(2,1)} %bitcast.47, bf16[2,1536,896]{2,1,0:T(8,128)(2,1)} %bitcast.39, bf16[2,1536,896]{2,1,0:T(8,128)(2,1)} %bitcast.40), custom_call_target="tpu_custom_call" | custom-call | tf_op jit(solution)/shard_map/project/pallas_call | solution.py:176
  144.3 8.6 %reduce-scatter.3.cloned.1.call-done.summed = bf16[392,512]{1,0:T(8,128)(2,1)} async-done(((bf16[3136,512]{1,0:T(8,128)(2,1)}), bf16[392,512]{1,0:T(8,128)(2,1)}) %reduce-scatter.3.cloned.1.call-update) | async-done | bytes 401424 | tf_op jit(solution)/shard_map/reduce_scatter | solution.py:345
  157.4 3.3 %collective-permute-done.8.refs_1_ = bf16[192,512]{1,0:T(8,128)(2,1)S(1)} collective-permute-done((bf16[192,512]{1,0:T(8,128)(2,1)}, bf16[192,512]{1,0:T(8,128)(2,1)S(1)}, u32[]{:S(2)}, u32[]{:S(2)}) %collective-permute-start.8) | collective-permute-done | bytes 196640 | tf_op jit(solution)/shard_map/ppermute | solution.py:336
  169.3 52.5 %reduce-scatter.5.cloned.1.call-done.summed = bf16[392,768]{1,0:T(8,128)(2,1)} async-done(((bf16[3136,768]{1,0:T(8,128)(2,1)}), bf16[392,768]{1,0:T(8,128)(2,1)}) %reduce-scatter.5.cloned.1.call-update) | async-done | bytes 602128 | tf_op jit(solution)/shard_map/reduce_scatter | solution.py:345
  230.0 5.0 %collective-permute-done.14.refs_7_ = bf16[96,512]{1,0:T(8,128)(2,1)S(1)} collective-permute-done((bf16[96,512]{1,0:T(8,128)(2,1)S(1)}, bf16[96,512]{1,0:T(8,128)(2,1)S(1)}, u32[]{:S(2)}, u32[]{:S(2)}) %collective-permute-start.14) | collective-permute-done | bytes 98336 | tf_op jit(solution)/shard_map/ppermute | solution.py:336
  236.7 5.9 %down.2 = bf16[512,896]{1,0:T(8,128)(2,1)} custom-call(s32[8]{0:T(128)} %stack.80.places, bf16[192,512]{1,0:T(8,128)(2,1)} %activate.2.refs_0_, bf16[192,512]{1,0:T(8,128)(2,1)} %copy-done.20, bf16[192,512]{1,0:T(8,128)(2,1)} %copy-done.22, bf16[192,512]{1,0:T(8,128)(2,1)} %copy-done.14, bf16[192,512]{1,0:T(8,128)(2,1)} %copy-done.21, ...), custom_call_target="tpu_custom_call" | custom-call | tf_op jit(solution)/shard_map/down/pallas_call | solution.py:230
  242.7 8.2 %all-to-all-start.2 = ((bf16[32,16,896]{2,1,0:T(8,128)(2,1)}), bf16[32,16,896]{2,1,0:T(8,128)(2,1)S(1)}, u32[]{:S(2)}, u32[]{:S(2)}) async-start(bf16[32,16,896]{2,1,0:T(8,128)(2,1)} %bitcast.49), calls=%async_computation.3 | async-start | bytes 1835008 | tf_op jit(solution)/shard_map/all_to_all | solution.py:330
  253.7 6.9 %collective-permute-done.17.refs_2_ = bf16[192,768]{1,0:T(8,128)(2,1)S(1)} collective-permute-done((bf16[192,768]{1,0:T(8,128)(2,1)S(1)}, bf16[192,768]{1,0:T(8,128)(2,1)S(1)}, u32[]{:S(2)}, u32[]{:S(2)}) %collective-permute-start.17) | collective-permute-done | bytes 294944 | tf_op jit(solution)/shard_map/ppermute | solution.py:336
  263.2 6.0 %collective-permute-done.18.refs_3_ = bf16[192,768]{1,0:T(8,128)(2,1)S(1)} collective-permute-done((bf16[192,768]{1,0:T(8,128)(2,1)S(1)}, bf16[192,768]{1,0:T(8,128)(2,1)S(1)}, u32[]{:S(2)}, u32[]{:S(2)}) %collective-permute-start.18) | collective-permute-done | bytes 294944 | tf_op jit(solution)/shard_map/ppermute | solution.py:336
  276.1 7.3 %down.3 = bf16[768,896]{1,0:T(8,128)(2,1)} custom-call(s32[8]{0:T(128)} %stack.80.places, bf16[192,768]{1,0:T(8,128)(2,1)} %activate.3.refs_0_, bf16[192,768]{1,0:T(8,128)(2,1)} %copy-done.16, bf16[192,768]{1,0:T(8,128)(2,1)} %copy-done.18, bf16[192,768]{1,0:T(8,128)(2,1)} %copy-done.7, bf16[192,768]{1,0:T(8,128)(2,1)} %copy-done.17, ...), custom_call_target="tpu_custom_call" | custom-call | tf_op jit(solution)/shard_map/down/pallas_call | solution.py:230
  283.4 10.0 %all-to-all-start.4 = ((bf16[32,24,896]{2,1,0:T(8,128)(2,1)}), bf16[32,24,896]{2,1,0:T(8,128)(2,1)S(1)}, u32[]{:S(2)}, u32[]{:S(2)}) async-start(bf16[32,24,896]{2,1,0:T(8,128)(2,1)} %bitcast.45), calls=%async_computation.6 | async-start | bytes 2752512 | tf_op jit(solution)/shard_map/all_to_all | solution.py:330
  295.8 17.3 %all-to-all-done.4 = bf16[32,24,896]{2,1,0:T(8,128)(2,1)S(1)} async-done(((bf16[32,24,896]{2,1,0:T(8,128)(2,1)}), bf16[32,24,896]{2,1,0:T(8,128)(2,1)S(1)}, u32[]{:S(2)}, u32[]{:S(2)}) %all-to-all-start.4) | async-done | bytes 1376288 | tf_op jit(solution)/shard_map/all_to_all | solution.py:330
  (130 shorter events, 65.2 us)
Async XLA Ops:
  7.7 13.2 %collective-permute-start = (bf16[2,128,896]{2,1,0:T(8,128)(2,1)S(1)}, bf16[2,128,896]{2,1,0:T(8,128)(2,1)S(1)}, u32[]{:S(2)}, u32[]{:S(2)}) collective-permute-start(bf16[2,128,896]{2,1,0:T(8,128)(2,1)S(1)} %pad_maximum_fusion.refs_0_), channel_id=1, source_target_pairs={{0,64},{8,72},{16,80},{24,88},{32,96},{40,104},{48,112},{56,120},{... | collective-permute-start | bytes 1376264 | tf_op jit(solution)/shard_map/ppermute | solution.py:304
  22.9 11.8 %collective-permute-start.1 = (bf16[2,128,896]{2,1,0:T(8,128)(2,1)S(1)}, bf16[2,128,896]{2,1,0:T(8,128)(2,1)S(1)}, u32[]{:S(2)}, u32[]{:S(2)}) collective-permute-start(bf16[2,128,896]{2,1,0:T(8,128)(2,1)S(1)} %get-tuple-element.22), channel_id=1, source_target_pairs={{0,16},{8,24},{16,32},{24,40},{32,48},{40,56},{48,0},{56,8},{64,80... | collective-permute-start | bytes 1376264 | tf_op jit(solution)/shard_map/ppermute | solution.py:299
  24.1 21.4 %collective-permute-start.2 = (bf16[2,128,896]{2,1,0:T(8,128)(2,1)S(1)}, bf16[2,128,896]{2,1,0:T(8,128)(2,1)S(1)}, u32[]{:S(2)}, u32[]{:S(2)}) collective-permute-start(bf16[2,128,896]{2,1,0:T(8,128)(2,1)S(1)} %get-tuple-element.21), channel_id=1, source_target_pairs={{0,32},{8,40},{16,48},{24,56},{32,0},{40,8},{48,16},{56,24},{64,96... | collective-permute-start | bytes 1376264 | tf_op jit(solution)/shard_map/ppermute | solution.py:299
  26.6 21.3 %collective-permute-start.3 = (bf16[2,128,896]{2,1,0:T(8,128)(2,1)S(1)}, bf16[2,128,896]{2,1,0:T(8,128)(2,1)S(1)}, u32[]{:S(2)}, u32[]{:S(2)}) collective-permute-start(bf16[2,128,896]{2,1,0:T(8,128)(2,1)S(1)} %get-tuple-element.20), channel_id=1, source_target_pairs={{0,48},{8,56},{16,0},{24,8},{32,16},{40,24},{48,32},{56,40},{64,11... | collective-permute-start | bytes 1376264 | tf_op jit(solution)/shard_map/ppermute | solution.py:299
  27.7 38.3 %collective-permute-start.4 = (bf16[2,128,896]{2,1,0:T(8,128)(2,1)}, bf16[2,128,896]{2,1,0:T(8,128)(2,1)S(1)}, u32[]{:S(2)}, u32[]{:S(2)}) collective-permute-start(bf16[2,128,896]{2,1,0:T(8,128)(2,1)} %get-tuple-element.19), channel_id=1, source_target_pairs={{0,8},{8,0},{16,24},{24,16},{32,40},{40,32},{48,56},{56,48},{64,72... | collective-permute-start | bytes 1376264 | tf_op jit(solution)/shard_map/ppermute | solution.py:302
  34.7 31.4 %collective-permute-start.5 = (bf16[2,128,896]{2,1,0:T(8,128)(2,1)S(1)}, bf16[2,128,896]{2,1,0:T(8,128)(2,1)S(1)}, u32[]{:S(2)}, u32[]{:S(2)}) collective-permute-start(bf16[2,128,896]{2,1,0:T(8,128)(2,1)S(1)} %collective-permute-done.1.refs_1_), channel_id=1, source_target_pairs={{0,8},{8,0},{16,24},{24,16},{32,40},{40,32},{48,56},{56,48},{64,72... | collective-permute-start | bytes 1376264 | tf_op jit(solution)/shard_map/ppermute | solution.py:302
  45.5 20.6 %collective-permute-start.6 = (bf16[2,128,896]{2,1,0:T(8,128)(2,1)S(1)}, bf16[2,128,896]{2,1,0:T(8,128)(2,1)}, u32[]{:S(2)}, u32[]{:S(2)}) collective-permute-start(bf16[2,128,896]{2,1,0:T(8,128)(2,1)S(1)} %collective-permute-done.2.refs_2_), channel_id=1, source_target_pairs={{0,8},{8,0},{16,24},{24,16},{32,40},{40,32},{48,56},{56,48},{64,72... | collective-permute-start | bytes 1376264 | tf_op jit(solution)/shard_map/ppermute | solution.py:302
  47.9 18.2 %collective-permute-start.7 = (bf16[2,128,896]{2,1,0:T(8,128)(2,1)S(1)}, bf16[2,128,896]{2,1,0:T(8,128)(2,1)}, u32[]{:S(2)}, u32[]{:S(2)}) collective-permute-start(bf16[2,128,896]{2,1,0:T(8,128)(2,1)S(1)} %collective-permute-done.3.refs_3_), channel_id=1, source_target_pairs={{0,8},{8,0},{16,24},{24,16},{32,40},{40,32},{48,56},{56,48},{64,72... | collective-permute-start | bytes 1376264 | tf_op jit(solution)/shard_map/ppermute | solution.py:302
  48.9 16.2 %all-to-all-start = ((bf16[32,2,2,896]{3,2,1,0:T(2,128)(2,1)}), bf16[32,2,2,896]{3,2,1,0:T(2,128)(2,1)S(1)}, u32[]{:S(2)}, u32[]{:S(2)}) async-start(bf16[32,2,2,896]{3,2,1,0:T(2,128)(2,1)} %broadcast_in_dim.10), calls=%async_computation | async-start | bytes 458752 | tf_op jit(solution)/shard_map/all_to_all | solution.py:318
  76.9 20.4 %all-to-all-start.1 = ((bf16[32,16,896]{2,1,0:T(8,128)(2,1)}), bf16[32,16,896]{2,1,0:T(8,128)(2,1)S(1)}, u32[]{:S(2)}, u32[]{:S(2)}) async-start(bf16[32,16,896]{2,1,0:T(8,128)(2,1)} %bitcast.58), calls=%async_computation.1 | async-start | bytes 1835008 | tf_op jit(solution)/shard_map/all_to_all | solution.py:330
  81.6 71.2 %reduce-scatter.3.cloned.1.call-start = ((), (), s32[]{:S(2)}) async-start(), calls=%async_computation.7 | async-start | bytes 3612672 | tf_op jit(solution)/shard_map/reduce_scatter | solution.py:345
  106.0 115.8 %reduce-scatter.5.cloned.1.call-start = ((), (), s32[]{:S(2)}) async-start(), calls=%async_computation.8 | async-start | bytes 5419008 | tf_op jit(solution)/shard_map/reduce_scatter | solution.py:345
  166.4 60.1 %collective-permute-start.10 = (bf16[192,512]{1,0:T(8,128)(2,1)S(1)}, bf16[192,512]{1,0:T(8,128)(2,1)S(1)}, u32[]{:S(2)}, u32[]{:S(2)}) collective-permute-start(bf16[192,512]{1,0:T(8,128)(2,1)S(1)} %collective-permute-done.9.refs_2_), channel_id=1, source_target_pairs={{0,1},{1,2},{2,3},{3,4},{4,5},{5,6},{6,7},{7,0},{8,9},{9,10},{10,1... | collective-permute-start | bytes 589832 | tf_op jit(solution)/shard_map/ppermute | solution.py:336
  166.4 60.8 %collective-permute-start.13 = (bf16[192,512]{1,0:T(8,128)(2,1)S(1)}, bf16[192,512]{1,0:T(8,128)(2,1)S(1)}, u32[]{:S(2)}, u32[]{:S(2)}) collective-permute-start(bf16[192,512]{1,0:T(8,128)(2,1)S(1)} %collective-permute-done.12.refs_5_), channel_id=1, source_target_pairs={{0,7},{1,0},{2,1},{3,2},{4,3},{5,4},{6,5},{7,6},{8,15},{9,8},{10,9... | collective-permute-start | bytes 589832 | tf_op jit(solution)/shard_map/ppermute | solution.py:337
  223.8 27.1 %collective-permute-start.16 = (bf16[192,768]{1,0:T(8,128)(2,1)}, bf16[192,768]{1,0:T(8,128)(2,1)S(1)}, u32[]{:S(2)}, u32[]{:S(2)}) collective-permute-start(bf16[192,768]{1,0:T(8,128)(2,1)} %activate.3.refs_0_), channel_id=1, source_target_pairs={{0,1},{1,2},{2,3},{3,4},{4,5},{5,6},{6,7},{7,0},{8,9},{9,10},{10,1... | collective-permute-start | bytes 884744 | tf_op jit(solution)/shard_map/ppermute | solution.py:336
  225.2 28.1 %collective-permute-start.19 = (bf16[192,768]{1,0:T(8,128)(2,1)}, bf16[192,768]{1,0:T(8,128)(2,1)S(1)}, u32[]{:S(2)}, u32[]{:S(2)}) collective-permute-start(bf16[192,768]{1,0:T(8,128)(2,1)} %activate.3.refs_0_), channel_id=1, source_target_pairs={{0,7},{1,0},{2,1},{3,2},{4,3},{5,4},{6,5},{7,6},{8,15},{9,8},{10,9... | collective-permute-start | bytes 884744 | tf_op jit(solution)/shard_map/ppermute | solution.py:337
  226.5 8.6 %collective-permute-start.14 = (bf16[96,512]{1,0:T(8,128)(2,1)S(1)}, bf16[96,512]{1,0:T(8,128)(2,1)S(1)}, u32[]{:S(2)}, u32[]{:S(2)}) collective-permute-start(bf16[96,512]{1,0:T(8,128)(2,1)S(1)} %slice.16), channel_id=1, source_target_pairs={{0,1},{1,2},{2,3},{3,4},{4,5},{5,6},{6,7},{7,0},{8,9},{9,10},{10,1... | collective-permute-start | bytes 294920 | tf_op jit(solution)/shard_map/ppermute | solution.py:336
  227.2 8.9 %collective-permute-start.15 = (bf16[96,512]{1,0:T(8,128)(2,1)S(1)}, bf16[96,512]{1,0:T(8,128)(2,1)S(1)}, u32[]{:S(2)}, u32[]{:S(2)}) collective-permute-start(bf16[96,512]{1,0:T(8,128)(2,1)S(1)} %slice.17), channel_id=1, source_target_pairs={{0,7},{1,0},{2,1},{3,2},{4,3},{5,4},{6,5},{7,6},{8,15},{9,8},{10,9... | collective-permute-start | bytes 294920 | tf_op jit(solution)/shard_map/ppermute | solution.py:337
  242.7 40.7 %all-to-all-start.2 = ((bf16[32,16,896]{2,1,0:T(8,128)(2,1)}), bf16[32,16,896]{2,1,0:T(8,128)(2,1)S(1)}, u32[]{:S(2)}, u32[]{:S(2)}) async-start(bf16[32,16,896]{2,1,0:T(8,128)(2,1)} %bitcast.49), calls=%async_computation.3 | async-start | bytes 1835008 | tf_op jit(solution)/shard_map/all_to_all | solution.py:330
  250.9 9.6 %collective-permute-start.17 = (bf16[192,768]{1,0:T(8,128)(2,1)S(1)}, bf16[192,768]{1,0:T(8,128)(2,1)S(1)}, u32[]{:S(2)}, u32[]{:S(2)}) collective-permute-start(bf16[192,768]{1,0:T(8,128)(2,1)S(1)} %collective-permute-done.16.refs_1_), channel_id=1, source_target_pairs={{0,1},{1,2},{2,3},{3,4},{4,5},{5,6},{6,7},{7,0},{8,9},{9,10},{10,1... | collective-permute-start | bytes 884744 | tf_op jit(solution)/shard_map/ppermute | solution.py:336
  253.2 8.3 %collective-permute-start.20 = (bf16[192,768]{1,0:T(8,128)(2,1)S(1)}, bf16[192,768]{1,0:T(8,128)(2,1)S(1)}, u32[]{:S(2)}, u32[]{:S(2)}) collective-permute-start(bf16[192,768]{1,0:T(8,128)(2,1)S(1)} %collective-permute-done.19.refs_4_), channel_id=1, source_target_pairs={{0,7},{1,0},{2,1},{3,2},{4,3},{5,4},{6,5},{7,6},{8,15},{9,8},{10,9... | collective-permute-start | bytes 884744 | tf_op jit(solution)/shard_map/ppermute | solution.py:337
  260.6 8.7 %collective-permute-start.18 = (bf16[192,768]{1,0:T(8,128)(2,1)S(1)}, bf16[192,768]{1,0:T(8,128)(2,1)S(1)}, u32[]{:S(2)}, u32[]{:S(2)}) collective-permute-start(bf16[192,768]{1,0:T(8,128)(2,1)S(1)} %collective-permute-done.17.refs_2_), channel_id=1, source_target_pairs={{0,1},{1,2},{2,3},{3,4},{4,5},{5,6},{6,7},{7,0},{8,9},{9,10},{10,1... | collective-permute-start | bytes 884744 | tf_op jit(solution)/shard_map/ppermute | solution.py:336
  261.6 8.0 %collective-permute-start.21 = (bf16[192,768]{1,0:T(8,128)(2,1)S(1)}, bf16[192,768]{1,0:T(8,128)(2,1)S(1)}, u32[]{:S(2)}, u32[]{:S(2)}) collective-permute-start(bf16[192,768]{1,0:T(8,128)(2,1)S(1)} %collective-permute-done.20.refs_5_), channel_id=1, source_target_pairs={{0,7},{1,0},{2,1},{3,2},{4,3},{5,4},{6,5},{7,6},{8,15},{9,8},{10,9... | collective-permute-start | bytes 884744 | tf_op jit(solution)/shard_map/ppermute | solution.py:337
  283.4 29.7 %all-to-all-start.4 = ((bf16[32,24,896]{2,1,0:T(8,128)(2,1)}), bf16[32,24,896]{2,1,0:T(8,128)(2,1)S(1)}, u32[]{:S(2)}, u32[]{:S(2)}) async-start(bf16[32,24,896]{2,1,0:T(8,128)(2,1)} %bitcast.45), calls=%async_computation.6 | async-start | bytes 2752512 | tf_op jit(solution)/shard_map/all_to_all | solution.py:330
  (37 other events, 772.5 us)
Sparse Core Ops, SparseCore 0:
  106.1 46.7 reduce-scatter.2
  155.4 66.3 reduce-scatter.4

commit v4 on v3

--- a/solution.py
+++ b/solution.py
@@ -242,6 +242,38 @@
     )(places, *acts, w)
 
 
+def down_some_kernel(places, *refs, which, start):
+    *acts, w, out = refs[1:] if start else refs
+    half = acts[0].shape[0]
+    picked = [w[pl.ds(pl.multiple_of(places[k] * half, 64), half), :] for k in which]
+    total = mm(
+        jnp.concatenate([a[...] for a in acts], axis=0), jnp.concatenate(picked, axis=0), 0, 0
+    )
+    if start:
+        total = total + refs[0][...]
+    out[...] = total.astype(out.dtype)
+
+
+def down_some(places, acts, w, which, start=None, tile=256):
+    rows = acts[0].shape[1]
+    hidden, features = w.shape
+    product = pl.BlockSpec((tile, features), lambda i, a: (i, 0))
+    before = [] if start is None else [start]
+    return pl.pallas_call(
+        functools.partial(down_some_kernel, which=which, start=bool(before)),
+        name="down_some",
+        grid_spec=pltpu.PrefetchScalarGridSpec(
+            num_scalar_prefetch=1,
+            grid=(rows // tile,),
+            in_specs=[product] * len(before)
+            + [pl.BlockSpec((a.shape[0], tile), lambda i, a: (0, i)) for a in acts]
+            + [pl.BlockSpec((hidden, features), lambda i, a: (0, 0))],
+            out_specs=product,
+        ),
+        out_shape=jax.ShapeDtypeStruct((rows, features), bf16 if before else f32),
+    )(places, *before, *acts, w)
+
+
 def combine_kernel(slot, ids, scores, x, back, out, *, base, slots):
     experts, tokens = slot.shape
     route_w = ROUTE_SCALE * scores[...] / jnp.sum(scores[...], axis=0, keepdims=True)
@@ -353,7 +385,13 @@
             rights.append(send_right(rights[-1]))
             lefts.append(send_left(lefts[-1]))
         top, bottom = send_right(rights[-1][:middle]), send_left(lefts[-1][middle:])
-        result = down(places, [*rights, *lefts[1:], top, bottom], w_down[0])
+        if c == 0:
+            result = down(places, [*rights, *lefts[1:], top, bottom], w_down[0])
+        else:
+            near = [*rights[:3], *lefts[1:3]]
+            result = down_some(places, near, w_down[0], (0, 1, 2, 4, 5))
+            last_blocks = [rights[3], lefts[3], top, bottom]
+            result = down_some(places, last_blocks, w_down[0], (3, 6, 7), result)
         back = exchanged(result, n)
         last = c == len(PARTS) - 1
         mixed = combine(

time: 326 us -> 328 us (level)
  Pallas kernels: 53 us -> 58.8 us
    pallas_call x0 -> x2, Pallas kernels: none -> 13 us  [down_some(): pl.pallas_call(functools.partial(down_some_kernel, which=which, start=boo...]
    pallas_call x2 -> x1, Pallas kernels: 13.2 us -> 5.96 us  [down(): pl.pallas_call(down_kernel, name='down', grid_spec=pltpu.PrefetchScalarGr...]
  transfers between devices with their start and end apart: 30 -> 30, of which waited for: 15 -> 14; matrix products, arithmetic and copies ran while one was open for 6% -> 6% of each run, Pallas kernels for 10% -> 12%
where the time goes in v4:
time: 328 us; the launch traced here: 326 us
  waiting for transfers between devices  128 us (39%)
  starting transfers between devices  69.4 us (21%)
  Pallas kernels  58.8 us (18%)
  blocking collectives  27.5 us (8%)
  local copies, waits for them, and re-layouts  25.7 us (8%)
  between operations  13.8 us (4%)
    reduce_scatter x2, waiting for transfers between devices, local(): lax.psum_scatter(whole.reshape(-1, peers * n), 'exp', scatter_dimension=0...  61.1 us
    all_to_all x1, blocking collectives, exchanged(): lax.all_to_all(x.reshape(peers, n, features), 'seq', split_axis=0, concat...  27.5 us
    ppermute x8, waiting for transfers between devices, local(): send_right = lambda x: lax.ppermute(x, 'exp', to_right)  24.3 us
    all_to_all x3, starting transfers between devices, exchanged(): lax.all_to_all(x.reshape(peers, n, features), 'seq', split_axis=0, concat...  22.3 us
    unnamed x64, local copies, waits for them, and re-layouts  20.7 us
    all_to_all x3, waiting for transfers between devices, exchanged(): lax.all_to_all(x.reshape(peers, n, features), 'seq', split_axis=0, concat...  17.8 us
    pallas_call x2, Pallas kernels, project(): pl.pallas_call(project_kernel, name='project', grid=(shards // pair,), in...  17.1 us
    ppermute x8, starting transfers between devices, local(): send_left = lambda x: lax.ppermute(x, 'exp', to_left)  16.6 us
  transfers between devices with their start and end apart: 30, of which 14 were waited for; matrix products, arithmetic and copies ran while one was open for 6% of the time, Pallas kernels for 12%

profile of v4, /device:TPU:1, one launch (start us, length us, event | category | flops | bytes accessed | tf_op | source)
XLA Modules:
  0.0 326.5 jit_solution(17380786893126509177)
XLA Ops:
  7.7 4.0 %collective-permute-start = (bf16[2,128,896]{2,1,0:T(8,128)(2,1)S(1)}, bf16[2,128,896]{2,1,0:T(8,128)(2,1)S(1)}, u32[]{:S(2)}, u32[]{:S(2)}) collective-permute-start(bf16[2,128,896]{2,1,0:T(8,128)(2,1)S(1)} %pad_maximum_fusion.refs_0_), channel_id=1, source_target_pairs={{0,64},{8,72},{16,80},{24,88},{32,96},{40,104},{48,112},{56,120},{... | collective-permute-start | bytes 1376264 | tf_op jit(solution)/shard_map/ppermute | solution.py:336
  11.8 9.1 %collective-permute-done = bf16[2,128,896]{2,1,0:T(8,128)(2,1)S(1)} collective-permute-done((bf16[2,128,896]{2,1,0:T(8,128)(2,1)S(1)}, bf16[2,128,896]{2,1,0:T(8,128)(2,1)S(1)}, u32[]{:S(2)}, u32[]{:S(2)}) %collective-permute-start) | collective-permute-done | bytes 458784 | tf_op jit(solution)/shard_map/ppermute | solution.py:336
  30.1 4.6 %collective-permute-done.1.refs_1_ = bf16[2,128,896]{2,1,0:T(8,128)(2,1)S(1)} collective-permute-done((bf16[2,128,896]{2,1,0:T(8,128)(2,1)S(1)}, bf16[2,128,896]{2,1,0:T(8,128)(2,1)S(1)}, u32[]{:S(2)}, u32[]{:S(2)}) %collective-permute-start.1) | collective-permute-done | bytes 458784 | tf_op jit(solution)/shard_map/ppermute | solution.py:331
  34.7 3.4 %collective-permute-start.5 = (bf16[2,128,896]{2,1,0:T(8,128)(2,1)S(1)}, bf16[2,128,896]{2,1,0:T(8,128)(2,1)S(1)}, u32[]{:S(2)}, u32[]{:S(2)}) collective-permute-start(bf16[2,128,896]{2,1,0:T(8,128)(2,1)S(1)} %collective-permute-done.1.refs_1_), channel_id=1, source_target_pairs={{0,8},{8,0},{16,24},{24,16},{32,40},{40,32},{48,56},{56,48},{64,72... | collective-permute-start | bytes 1376264 | tf_op jit(solution)/shard_map/ppermute | solution.py:334
  38.1 7.4 %collective-permute-done.2.refs_2_ = bf16[2,128,896]{2,1,0:T(8,128)(2,1)S(1)} collective-permute-done((bf16[2,128,896]{2,1,0:T(8,128)(2,1)S(1)}, bf16[2,128,896]{2,1,0:T(8,128)(2,1)S(1)}, u32[]{:S(2)}, u32[]{:S(2)}) %collective-permute-start.2) | collective-permute-done | bytes 458784 | tf_op jit(solution)/shard_map/ppermute | solution.py:331
  48.9 7.6 %all-to-all-start = ((bf16[32,2,2,896]{3,2,1,0:T(2,128)(2,1)}), bf16[32,2,2,896]{3,2,1,0:T(2,128)(2,1)S(1)}, u32[]{:S(2)}, u32[]{:S(2)}) async-start(bf16[32,2,2,896]{3,2,1,0:T(2,128)(2,1)} %broadcast_in_dim.10), calls=%async_computation | async-start | bytes 458752 | tf_op jit(solution)/shard_map/all_to_all | solution.py:350
  58.6 3.8 %tables.1 = (f32[128,1024]{1,0:T(8,128)}, f32[128,64]{1,0:T(8,128)}, bf16[1280,128]{1,0:T(8,128)(2,1)}, f32[32,128]{1,0:T(8,128)}) custom-call(s32[9]{0:T(128)} %stack.65.meta, s32[128,8]{1,0:T(8,128)} %bitcast.61, s32[8,128]{1,0:T(8,128)} %bitcast.62), custom_call_target="tpu_custom_call" | custom-call | tf_op jit(solution)/shard_map/tables/pallas_call | solution.py:80
  67.0 9.9 %attend.1 = (bf16[128,896]{1,0:T(8,128)(2,1)}, bf16[512,896]{1,0:T(8,128)(2,1)}, bf16[768,896]{1,0:T(8,128)(2,1)}) custom-call(f32[128,1024]{1,0:T(8,128)} %get-tuple-element.13.bias, f32[128,64]{1,0:T(8,128)} %get-tuple-element.14.cbias, bf16[1280,128]{1,0:T(8,128)(2,1)} %get-tuple-element.15.onehot, f32[128,14]{1,0:T(8,128)} %copy.18.gates, ...), custom_call_target="tpu_custom_call" | custom-call | tf_op jit(solution)/shard_map/attend/pallas_call | solution.py:141
  76.9 4.7 %all-to-all-start.1 = ((bf16[32,16,896]{2,1,0:T(8,128)(2,1)}), bf16[32,16,896]{2,1,0:T(8,128)(2,1)S(1)}, u32[]{:S(2)}, u32[]{:S(2)}) async-start(bf16[32,16,896]{2,1,0:T(8,128)(2,1)} %bitcast.59), calls=%async_computation.1 | async-start | bytes 1835008 | tf_op jit(solution)/shard_map/all_to_all | solution.py:362
  82.3 14.4 %copy.19 = bf16[1,896,2,1536]{1,3,2,0:T(8,128)(2,1)} copy(bf16[1,896,2,1536]{3,2,1,0:T(2,128)(2,1)} %param.18) | data formatting | bytes 11010048 | tf_op args[8]
  98.3 7.6 %project.2 = bf16[8,392,512]{2,1,0:T(8,128)(2,1)} custom-call(f32[1,896]{1,0:T(1,128)} %broadcast_in_dim.11.gain, bf16[512,896]{1,0:T(8,128)(2,1)} %bitcast.51, bf16[2,1536,896]{2,1,0:T(8,128)(2,1)} %bitcast.37, bf16[2,1536,896]{2,1,0:T(8,128)(2,1)} %bitcast.38), custom_call_target="tpu_custom_call" | custom-call | tf_op jit(solution)/shard_map/project/pallas_call | solution.py:176
  107.3 27.5 %all_to_all.25 = bf16[32,24,896]{2,1,0:T(8,128)(2,1)} all-to-all(bf16[32,24,896]{2,1,0:T(8,128)(2,1)S(1)} %bitcast.58), channel_id=1, replica_groups=mesh['seq'=32,'exp'=8] {'seq'}, dimensions={0} | all-to-all | bytes 2752512 | tf_op jit(solution)/shard_map/all_to_all | solution.py:362
  134.8 9.5 %project.3 = bf16[8,392,768]{2,1,0:T(8,128)(2,1)} custom-call(f32[1,896]{1,0:T(1,128)} %broadcast_in_dim.11.gain, bf16[768,896]{1,0:T(8,128)(2,1)} %bitcast.48, bf16[2,1536,896]{2,1,0:T(8,128)(2,1)} %bitcast.39, bf16[2,1536,896]{2,1,0:T(8,128)(2,1)} %bitcast.40), custom_call_target="tpu_custom_call" | custom-call | tf_op jit(solution)/shard_map/project/pallas_call | solution.py:176
  144.3 8.6 %reduce-scatter.3.cloned.1.call-done.summed = bf16[392,512]{1,0:T(8,128)(2,1)} async-done(((bf16[3136,512]{1,0:T(8,128)(2,1)}), bf16[392,512]{1,0:T(8,128)(2,1)}) %reduce-scatter.3.cloned.1.call-update) | async-done | bytes 401424 | tf_op jit(solution)/shard_map/reduce_scatter | solution.py:377
  169.3 52.5 %reduce-scatter.5.cloned.1.call-done.summed = bf16[392,768]{1,0:T(8,128)(2,1)} async-done(((bf16[3136,768]{1,0:T(8,128)(2,1)}), bf16[392,768]{1,0:T(8,128)(2,1)}) %reduce-scatter.5.cloned.1.call-update) | async-done | bytes 602128 | tf_op jit(solution)/shard_map/reduce_scatter | solution.py:377
  230.0 5.1 %collective-permute-done.14.refs_7_ = bf16[96,512]{1,0:T(8,128)(2,1)S(1)} collective-permute-done((bf16[96,512]{1,0:T(8,128)(2,1)S(1)}, bf16[96,512]{1,0:T(8,128)(2,1)S(1)}, u32[]{:S(2)}, u32[]{:S(2)}) %collective-permute-start.14) | collective-permute-done | bytes 98336 | tf_op jit(solution)/shard_map/ppermute | solution.py:368
  236.7 6.0 %down.1 = bf16[512,896]{1,0:T(8,128)(2,1)} custom-call(s32[8]{0:T(128)} %stack.80.places, bf16[192,512]{1,0:T(8,128)(2,1)} %activate.2.refs_0_, bf16[192,512]{1,0:T(8,128)(2,1)} %copy-done.20, bf16[192,512]{1,0:T(8,128)(2,1)} %copy-done.22, bf16[192,512]{1,0:T(8,128)(2,1)} %copy-done.14, bf16[192,512]{1,0:T(8,128)(2,1)} %copy-done.21, ...), custom_call_target="tpu_custom_call" | custom-call | tf_op jit(solution)/shard_map/down/pallas_call | solution.py:230
  242.7 8.2 %all-to-all-start.2 = ((bf16[32,16,896]{2,1,0:T(8,128)(2,1)}), bf16[32,16,896]{2,1,0:T(8,128)(2,1)S(1)}, u32[]{:S(2)}, u32[]{:S(2)}) async-start(bf16[32,16,896]{2,1,0:T(8,128)(2,1)} %bitcast.50), calls=%async_computation.3 | async-start | bytes 1835008 | tf_op jit(solution)/shard_map/all_to_all | solution.py:362
  253.7 6.9 %collective-permute-done.17.refs_2_ = bf16[192,768]{1,0:T(8,128)(2,1)S(1)} collective-permute-done((bf16[192,768]{1,0:T(8,128)(2,1)S(1)}, bf16[192,768]{1,0:T(8,128)(2,1)S(1)}, u32[]{:S(2)}, u32[]{:S(2)}) %collective-permute-start.17) | collective-permute-done | bytes 294944 | tf_op jit(solution)/shard_map/ppermute | solution.py:368
  263.3 6.0 %collective-permute-done.20.refs_1_ = bf16[192,768]{1,0:T(8,128)(2,1)S(1)} collective-permute-done((bf16[192,768]{1,0:T(8,128)(2,1)S(1)}, bf16[192,768]{1,0:T(8,128)(2,1)S(1)}, u32[]{:S(2)}, u32[]{:S(2)}) %collective-permute-start.20) | collective-permute-done | bytes 294944 | tf_op jit(solution)/shard_map/ppermute | solution.py:368
  272.4 6.7 %down_some.2.refs_0_ = f32[768,896]{1,0:T(8,128)} custom-call(s32[8]{0:T(128)} %stack.80.places, bf16[192,768]{1,0:T(8,128)(2,1)} %activate.3.refs_0_, bf16[192,768]{1,0:T(8,128)(2,1)} %copy-done.16, bf16[192,768]{1,0:T(8,128)(2,1)} %copy-done.18, bf16[192,768]{1,0:T(8,128)(2,1)} %copy-done.17, bf16[192,768]{1,0:T(8,128)(2,1)} %copy-done.19, ...), custom_call_target="tpu_custom_call" | custom-call | tf_op jit(solution)/shard_map/down_some/pallas_call | solution.py:262
  280.4 6.3 %down_some.3 = bf16[768,896]{1,0:T(8,128)(2,1)} custom-call(s32[8]{0:T(128)} %stack.80.places, f32[768,896]{1,0:T(8,128)} %down_some.2.refs_0_, bf16[192,768]{1,0:T(8,128)(2,1)} %copy-done.7, bf16[192,768]{1,0:T(8,128)(2,1)} %copy-done.8, bf16[96,768]{1,0:T(8,128)(2,1)} %copy-done.24, bf16[96,768]{1,0:T(8,128)(2,1)} %copy-done.25, bf16[1536,896]{1,0:T(8,128)(2,1)} %bitcast.43), custom_call_target="tpu_custom_call" | custom-call | tf_op jit(solution)/shard_map/down_some/pallas_call | solution.py:262
  286.7 9.3 %all-to-all-start.4 = ((bf16[32,24,896]{2,1,0:T(8,128)(2,1)}), bf16[32,24,896]{2,1,0:T(8,128)(2,1)S(1)}, u32[]{:S(2)}, u32[]{:S(2)}) async-start(bf16[32,24,896]{2,1,0:T(8,128)(2,1)} %bitcast.47), calls=%async_computation.6 | async-start | bytes 2752512 | tf_op jit(solution)/shard_map/all_to_all | solution.py:362
  298.6 17.2 %all-to-all-done.4 = bf16[32,24,896]{2,1,0:T(8,128)(2,1)S(1)} async-done(((bf16[32,24,896]{2,1,0:T(8,128)(2,1)}), bf16[32,24,896]{2,1,0:T(8,128)(2,1)S(1)}, u32[]{:S(2)}, u32[]{:S(2)}) %all-to-all-start.4) | async-done | bytes 1376288 | tf_op jit(solution)/shard_map/all_to_all | solution.py:362
  (131 shorter events, 66.1 us)
Async XLA Ops:
  7.7 13.2 %collective-permute-start = (bf16[2,128,896]{2,1,0:T(8,128)(2,1)S(1)}, bf16[2,128,896]{2,1,0:T(8,128)(2,1)S(1)}, u32[]{:S(2)}, u32[]{:S(2)}) collective-permute-start(bf16[2,128,896]{2,1,0:T(8,128)(2,1)S(1)} %pad_maximum_fusion.refs_0_), channel_id=1, source_target_pairs={{0,64},{8,72},{16,80},{24,88},{32,96},{40,104},{48,112},{56,120},{... | collective-permute-start | bytes 1376264 | tf_op jit(solution)/shard_map/ppermute | solution.py:336
  22.9 11.8 %collective-permute-start.1 = (bf16[2,128,896]{2,1,0:T(8,128)(2,1)S(1)}, bf16[2,128,896]{2,1,0:T(8,128)(2,1)S(1)}, u32[]{:S(2)}, u32[]{:S(2)}) collective-permute-start(bf16[2,128,896]{2,1,0:T(8,128)(2,1)S(1)} %get-tuple-element.22), channel_id=1, source_target_pairs={{0,16},{8,24},{16,32},{24,40},{32,48},{40,56},{48,0},{56,8},{64,80... | collective-permute-start | bytes 1376264 | tf_op jit(solution)/shard_map/ppermute | solution.py:331
  24.1 21.4 %collective-permute-start.2 = (bf16[2,128,896]{2,1,0:T(8,128)(2,1)S(1)}, bf16[2,128,896]{2,1,0:T(8,128)(2,1)S(1)}, u32[]{:S(2)}, u32[]{:S(2)}) collective-permute-start(bf16[2,128,896]{2,1,0:T(8,128)(2,1)S(1)} %get-tuple-element.21), channel_id=1, source_target_pairs={{0,32},{8,40},{16,48},{24,56},{32,0},{40,8},{48,16},{56,24},{64,96... | collective-permute-start | bytes 1376264 | tf_op jit(solution)/shard_map/ppermute | solution.py:331
  26.6 21.3 %collective-permute-start.3 = (bf16[2,128,896]{2,1,0:T(8,128)(2,1)S(1)}, bf16[2,128,896]{2,1,0:T(8,128)(2,1)S(1)}, u32[]{:S(2)}, u32[]{:S(2)}) collective-permute-start(bf16[2,128,896]{2,1,0:T(8,128)(2,1)S(1)} %get-tuple-element.20), channel_id=1, source_target_pairs={{0,48},{8,56},{16,0},{24,8},{32,16},{40,24},{48,32},{56,40},{64,11... | collective-permute-start | bytes 1376264 | tf_op jit(solution)/shard_map/ppermute | solution.py:331
  27.7 38.3 %collective-permute-start.4 = (bf16[2,128,896]{2,1,0:T(8,128)(2,1)}, bf16[2,128,896]{2,1,0:T(8,128)(2,1)S(1)}, u32[]{:S(2)}, u32[]{:S(2)}) collective-permute-start(bf16[2,128,896]{2,1,0:T(8,128)(2,1)} %get-tuple-element.19), channel_id=1, source_target_pairs={{0,8},{8,0},{16,24},{24,16},{32,40},{40,32},{48,56},{56,48},{64,72... | collective-permute-start | bytes 1376264 | tf_op jit(solution)/shard_map/ppermute | solution.py:334
  34.7 31.4 %collective-permute-start.5 = (bf16[2,128,896]{2,1,0:T(8,128)(2,1)S(1)}, bf16[2,128,896]{2,1,0:T(8,128)(2,1)S(1)}, u32[]{:S(2)}, u32[]{:S(2)}) collective-permute-start(bf16[2,128,896]{2,1,0:T(8,128)(2,1)S(1)} %collective-permute-done.1.refs_1_), channel_id=1, source_target_pairs={{0,8},{8,0},{16,24},{24,16},{32,40},{40,32},{48,56},{56,48},{64,72... | collective-permute-start | bytes 1376264 | tf_op jit(solution)/shard_map/ppermute | solution.py:334
  45.5 20.6 %collective-permute-start.6 = (bf16[2,128,896]{2,1,0:T(8,128)(2,1)S(1)}, bf16[2,128,896]{2,1,0:T(8,128)(2,1)}, u32[]{:S(2)}, u32[]{:S(2)}) collective-permute-start(bf16[2,128,896]{2,1,0:T(8,128)(2,1)S(1)} %collective-permute-done.2.refs_2_), channel_id=1, source_target_pairs={{0,8},{8,0},{16,24},{24,16},{32,40},{40,32},{48,56},{56,48},{64,72... | collective-permute-start | bytes 1376264 | tf_op jit(solution)/shard_map/ppermute | solution.py:334
  47.9 18.2 %collective-permute-start.7 = (bf16[2,128,896]{2,1,0:T(8,128)(2,1)S(1)}, bf16[2,128,896]{2,1,0:T(8,128)(2,1)}, u32[]{:S(2)}, u32[]{:S(2)}) collective-permute-start(bf16[2,128,896]{2,1,0:T(8,128)(2,1)S(1)} %collective-permute-done.3.refs_3_), channel_id=1, source_target_pairs={{0,8},{8,0},{16,24},{24,16},{32,40},{40,32},{48,56},{56,48},{64,72... | collective-permute-start | bytes 1376264 | tf_op jit(solution)/shard_map/ppermute | solution.py:334
  48.9 16.2 %all-to-all-start = ((bf16[32,2,2,896]{3,2,1,0:T(2,128)(2,1)}), bf16[32,2,2,896]{3,2,1,0:T(2,128)(2,1)S(1)}, u32[]{:S(2)}, u32[]{:S(2)}) async-start(bf16[32,2,2,896]{3,2,1,0:T(2,128)(2,1)} %broadcast_in_dim.10), calls=%async_computation | async-start | bytes 458752 | tf_op jit(solution)/shard_map/all_to_all | solution.py:350
  76.9 20.4 %all-to-all-start.1 = ((bf16[32,16,896]{2,1,0:T(8,128)(2,1)}), bf16[32,16,896]{2,1,0:T(8,128)(2,1)S(1)}, u32[]{:S(2)}, u32[]{:S(2)}) async-start(bf16[32,16,896]{2,1,0:T(8,128)(2,1)} %bitcast.59), calls=%async_computation.1 | async-start | bytes 1835008 | tf_op jit(solution)/shard_map/all_to_all | solution.py:362
  81.6 71.2 %reduce-scatter.3.cloned.1.call-start = ((), (), s32[]{:S(2)}) async-start(), calls=%async_computation.7 | async-start | bytes 3612672 | tf_op jit(solution)/shard_map/reduce_scatter | solution.py:377
  106.0 115.8 %reduce-scatter.5.cloned.1.call-start = ((), (), s32[]{:S(2)}) async-start(), calls=%async_computation.8 | async-start | bytes 5419008 | tf_op jit(solution)/shard_map/reduce_scatter | solution.py:377
  166.4 60.1 %collective-permute-start.10 = (bf16[192,512]{1,0:T(8,128)(2,1)S(1)}, bf16[192,512]{1,0:T(8,128)(2,1)S(1)}, u32[]{:S(2)}, u32[]{:S(2)}) collective-permute-start(bf16[192,512]{1,0:T(8,128)(2,1)S(1)} %collective-permute-done.9.refs_2_), channel_id=1, source_target_pairs={{0,1},{1,2},{2,3},{3,4},{4,5},{5,6},{6,7},{7,0},{8,9},{9,10},{10,1... | collective-permute-start | bytes 589832 | tf_op jit(solution)/shard_map/ppermute | solution.py:368
  166.4 60.8 %collective-permute-start.13 = (bf16[192,512]{1,0:T(8,128)(2,1)S(1)}, bf16[192,512]{1,0:T(8,128)(2,1)S(1)}, u32[]{:S(2)}, u32[]{:S(2)}) collective-permute-start(bf16[192,512]{1,0:T(8,128)(2,1)S(1)} %collective-permute-done.12.refs_5_), channel_id=1, source_target_pairs={{0,7},{1,0},{2,1},{3,2},{4,3},{5,4},{6,5},{7,6},{8,15},{9,8},{10,9... | collective-permute-start | bytes 589832 | tf_op jit(solution)/shard_map/ppermute | solution.py:369
  223.8 27.1 %collective-permute-start.16 = (bf16[192,768]{1,0:T(8,128)(2,1)}, bf16[192,768]{1,0:T(8,128)(2,1)S(1)}, u32[]{:S(2)}, u32[]{:S(2)}) collective-permute-start(bf16[192,768]{1,0:T(8,128)(2,1)} %activate.3.refs_0_), channel_id=1, source_target_pairs={{0,1},{1,2},{2,3},{3,4},{4,5},{5,6},{6,7},{7,0},{8,9},{9,10},{10,1... | collective-permute-start | bytes 884744 | tf_op jit(solution)/shard_map/ppermute | solution.py:368
  225.2 28.1 %collective-permute-start.18 = (bf16[192,768]{1,0:T(8,128)(2,1)}, bf16[192,768]{1,0:T(8,128)(2,1)S(1)}, u32[]{:S(2)}, u32[]{:S(2)}) collective-permute-start(bf16[192,768]{1,0:T(8,128)(2,1)} %activate.3.refs_0_), channel_id=1, source_target_pairs={{0,7},{1,0},{2,1},{3,2},{4,3},{5,4},{6,5},{7,6},{8,15},{9,8},{10,9... | collective-permute-start | bytes 884744 | tf_op jit(solution)/shard_map/ppermute | solution.py:369
  226.5 8.6 %collective-permute-start.14 = (bf16[96,512]{1,0:T(8,128)(2,1)S(1)}, bf16[96,512]{1,0:T(8,128)(2,1)S(1)}, u32[]{:S(2)}, u32[]{:S(2)}) collective-permute-start(bf16[96,512]{1,0:T(8,128)(2,1)S(1)} %slice.16), channel_id=1, source_target_pairs={{0,1},{1,2},{2,3},{3,4},{4,5},{5,6},{6,7},{7,0},{8,9},{9,10},{10,1... | collective-permute-start | bytes 294920 | tf_op jit(solution)/shard_map/ppermute | solution.py:368
  227.2 8.9 %collective-permute-start.15 = (bf16[96,512]{1,0:T(8,128)(2,1)S(1)}, bf16[96,512]{1,0:T(8,128)(2,1)S(1)}, u32[]{:S(2)}, u32[]{:S(2)}) collective-permute-start(bf16[96,512]{1,0:T(8,128)(2,1)S(1)} %slice.17), channel_id=1, source_target_pairs={{0,7},{1,0},{2,1},{3,2},{4,3},{5,4},{6,5},{7,6},{8,15},{9,8},{10,9... | collective-permute-start | bytes 294920 | tf_op jit(solution)/shard_map/ppermute | solution.py:369
  242.7 44.0 %all-to-all-start.2 = ((bf16[32,16,896]{2,1,0:T(8,128)(2,1)}), bf16[32,16,896]{2,1,0:T(8,128)(2,1)S(1)}, u32[]{:S(2)}, u32[]{:S(2)}) async-start(bf16[32,16,896]{2,1,0:T(8,128)(2,1)} %bitcast.50), calls=%async_computation.3 | async-start | bytes 1835008 | tf_op jit(solution)/shard_map/all_to_all | solution.py:362
  251.0 9.6 %collective-permute-start.17 = (bf16[192,768]{1,0:T(8,128)(2,1)S(1)}, bf16[192,768]{1,0:T(8,128)(2,1)S(1)}, u32[]{:S(2)}, u32[]{:S(2)}) collective-permute-start(bf16[192,768]{1,0:T(8,128)(2,1)S(1)} %collective-permute-done.16.refs_1_), channel_id=1, source_target_pairs={{0,1},{1,2},{2,3},{3,4},{4,5},{5,6},{6,7},{7,0},{8,9},{9,10},{10,1... | collective-permute-start | bytes 884744 | tf_op jit(solution)/shard_map/ppermute | solution.py:368
  260.6 8.7 %collective-permute-start.20 = (bf16[192,768]{1,0:T(8,128)(2,1)S(1)}, bf16[192,768]{1,0:T(8,128)(2,1)S(1)}, u32[]{:S(2)}, u32[]{:S(2)}) collective-permute-start(bf16[192,768]{1,0:T(8,128)(2,1)S(1)} %collective-permute-done.17.refs_2_), channel_id=1, source_target_pairs={{0,1},{1,2},{2,3},{3,4},{4,5},{5,6},{6,7},{7,0},{8,9},{9,10},{10,1... | collective-permute-start | bytes 884744 | tf_op jit(solution)/shard_map/ppermute | solution.py:368
  269.3 9.8 %collective-permute-start.22 = (bf16[96,768]{1,0:T(8,128)(2,1)S(1)}, bf16[96,768]{1,0:T(8,128)(2,1)S(1)}, u32[]{:S(2)}, u32[]{:S(2)}) collective-permute-start(bf16[96,768]{1,0:T(8,128)(2,1)S(1)} %slice.18), channel_id=1, source_target_pairs={{0,1},{1,2},{2,3},{3,4},{4,5},{5,6},{6,7},{7,0},{8,9},{9,10},{10,1... | collective-permute-start | bytes 442376 | tf_op jit(solution)/shard_map/ppermute | solution.py:368
  269.6 9.5 %collective-permute-start.23 = (bf16[96,768]{1,0:T(8,128)(2,1)S(1)}, bf16[96,768]{1,0:T(8,128)(2,1)S(1)}, u32[]{:S(2)}, u32[]{:S(2)}) collective-permute-start(bf16[96,768]{1,0:T(8,128)(2,1)S(1)} %slice.19), channel_id=1, source_target_pairs={{0,7},{1,0},{2,1},{3,2},{4,3},{5,4},{6,5},{7,6},{8,15},{9,8},{10,9... | collective-permute-start | bytes 442376 | tf_op jit(solution)/shard_map/ppermute | solution.py:369
  286.7 29.1 %all-to-all-start.4 = ((bf16[32,24,896]{2,1,0:T(8,128)(2,1)}), bf16[32,24,896]{2,1,0:T(8,128)(2,1)S(1)}, u32[]{:S(2)}, u32[]{:S(2)}) async-start(bf16[32,24,896]{2,1,0:T(8,128)(2,1)} %bitcast.47), calls=%async_computation.6 | async-start | bytes 2752512 | tf_op jit(solution)/shard_map/all_to_all | solution.py:362
  (37 other events, 776.3 us)
Sparse Core Ops, SparseCore 0:
  106.1 46.7 reduce-scatter.2
  155.4 66.3 reduce-scatter.4
